TPU v7x, 128 devices: a whole 4x4x4 slice. The times are simulated.
128 devices in a mesh: grp: 4 (over x_hi, core), reg: 32 (over z, x_lo, y).
Axes of the slice: x: 4 (x_hi: 2, x_lo: 2; x = x_hi * 2 + x_lo), y: 4, z: 4, core: 2. Of those that a mesh axis runs over, the one named last changes fastest.
Arguments:
- grain_pos: float32 [3, 2097152], P(None, ('grp', 'reg')), may hold values from -6 to 6
- grain_vel: float32 [3, 2097152], P(None, ('grp', 'reg')), may hold values from -6 to 6
- grain_vol: float32 [2097152], P(('grp', 'reg')), may hold values from 0.5 to 2
- drag_coef: float32 [2097152], P(('grp', 'reg')), may hold values from 0.2 to 2
- grain_count: int32 [128], P(('grp', 'reg')), may hold values from 0 to 16384, as said below
- contact_rows: int32 [8, 2097152], P(None, ('grp', 'reg')), may hold values from -1 to 255, as said below
- contact_stiff: float32 [8, 2097152], P(None, ('grp', 'reg')), may hold values from 0.05 to 0.5
- partner_block: int32 [16384], P(('grp', 'reg')), may hold values from 0 to 191, as said below
- halo_list: int32 [2, 524288], P(None, ('grp', 'reg')), may hold values from 0 to 16383, as said below
- grain_cell: int32 [2097152], P(('grp', 'reg')), may hold values from 0 to 127
- tile_cell_block: int32 [16384], P(('grp', 'reg')), may hold values from 0 to 2047
- pressure_old: float32 [128, 128, 512], P('reg'), may hold values from -6 to 6
- pressure_source: float32 [128, 128, 512], P('reg'), may hold values from -6 to 6
- solid_old: float32 [128, 128, 512], P('reg'), may hold values from 0 to 1.5
Outputs:
- new_vel: float32 [3, 2097152], P(None, ('grp', 'reg'))
Inputs may be any that keep to these rules, and one draw needn't show every extreme that they name: `grain_count`: devices of the last grp index hold no grains; a device's live grains fill its first slots; some device holds 16384. `contact_rows`: for a live grain in block t, entries 0 to 127 name grains of block t and entries 128 to 255 name grains of block partner_block[t]; every named grain is live; -1 marks an empty slot. Entries of slots that are not live carry no meaning. `partner_block`: blocks below 128 are the device's own, the next 32 are those received from the lower region, the last 32 those from the upper region; a block holding live grains never names a region that does not exist. `halo_list`: every entry names a live grain of its device where the device holds grains, else 0.
All inputs are finite; a program needn't handle non-finite values.
Results may differ from a plain program's by a relative error of at most 0.0003.
Values sent between devices are 32-bit elements; how exact they have to be, the bound alone decides.
A program may use at most 64 MiB of HBM per device.

v0:
```python
import jax
import jax.numpy as jnp
from jax import lax
from jax.sharding import PartitionSpec as P

BLOCK = 128
ITERS = 4
HALO = 4096


SPRING = 1.0
DAMPING = 0.5
TIME_STEP = 0.5


def with_halo(shard, sides, width):
    for axis, dim in sides:
        count, length = (lax.axis_size(axis), shard.shape[dim])
        up = [(i, (i + 1) % count) for i in range(count - 1)]
        down = [(j, i) for i, j in up]
        last = lax.slice_in_dim(shard, length - width, length, axis=dim)
        initial = lax.slice_in_dim(shard, 0, width, axis=dim)
        before = lax.ppermute(last, axis, up)
        after = lax.ppermute(initial, axis, down)
        shard = jnp.concatenate([before, shard, after], axis=dim)
    return shard


def neighbours(padded):
    summed = padded[2:, 1:-1, 1:-1] + padded[:-2, 1:-1, 1:-1]
    summed = summed + padded[1:-1, 2:, 1:-1] + padded[1:-1, :-2, 1:-1]
    return summed + padded[1:-1, 1:-1, 2:] + padded[1:-1, 1:-1, :-2]


def rim_whole(pressure):
    padded = with_halo(pressure, (("reg", 0),), 1)
    return jnp.pad(padded, ((0, 0), (1, 1), (1, 1)))


def relax(pressure, source, solid_before, solid_now, drag_sum, extend):
    porous = 1.0 / (1.0 + solid_now)
    diagonal = 6.0 * porous + drag_sum + 1.0
    driving = source + solid_now - solid_before
    for sweep_index in range(ITERS):
        pressure = (driving + porous * neighbours(extend(pressure))) / diagonal
    return (pressure, 1.0 / (porous + drag_sum))


def place_blocks(tile_rows, block_ids, block_count, grid_shape):
    placing = (block_ids[:, None] == lax.broadcasted_iota(jnp.int32, (1, block_count), 1)).astype(
        jnp.float32
    )
    placed = jnp.einsum("ltc,tb->lbc", tile_rows, placing, precision=lax.Precision.HIGHEST)
    return placed.reshape((tile_rows.shape[0],) + grid_shape)


def contact_forces(grain_state, extended, contact_rows, contact_stiff, partner_block):
    slots_here = grain_state.shape[1]
    tiles_here = slots_here // BLOCK
    per_step = 8
    slot_count = contact_rows.shape[0]
    partner = jnp.take(extended.reshape(6, -1, BLOCK), partner_block, axis=1)
    paired = jnp.concatenate([grain_state.reshape(6, tiles_here, BLOCK), partner], 2)
    rows_tiled = contact_rows.reshape(slot_count, tiles_here, BLOCK)
    stiff_tiled = contact_stiff.reshape(slot_count, tiles_here, BLOCK)
    columns = lax.broadcasted_iota(jnp.int32, (per_step, BLOCK, 2 * BLOCK), 2)

    def step_forces(step_index, forces):
        first_tile = step_index * per_step
        pair_step = lax.dynamic_slice_in_dim(paired, first_tile, per_step, 1)
        rows_step = lax.dynamic_slice_in_dim(rows_tiled, first_tile, per_step, 1)
        stiff_step = lax.dynamic_slice_in_dim(stiff_tiled, first_tile, per_step, 1)
        weights = jnp.zeros((per_step, BLOCK, 2 * BLOCK), jnp.float32)
        for slot_index in range(slot_count):
            weights = weights + jnp.where(
                rows_step[slot_index][:, :, None] == columns,
                stiff_step[slot_index][:, :, None],
                0.0,
            )
        summed = jnp.einsum("tij,ctj->cti", weights, pair_step, precision=lax.Precision.HIGHEST)
        stiff_total = jnp.sum(jnp.where(rows_step >= 0, stiff_step, 0.0), 0)
        own_rows = pair_step[:, :, :BLOCK]
        spring = SPRING * (stiff_total * own_rows[:3] - summed[:3])
        damper = DAMPING * (summed[3:] - stiff_total * own_rows[3:])
        return lax.dynamic_update_slice_in_dim(forces, spring + damper, first_tile, 1)

    zero_forces = jnp.zeros((3, tiles_here, BLOCK), jnp.float32)
    forces = lax.fori_loop(0, tiles_here // per_step, step_forces, zero_forces)
    return forces.reshape(3, slots_here)


def on_device(
    grain_pos,
    grain_vel,
    grain_vol,
    drag_coef,
    grain_count,
    contact_rows,
    contact_stiff,
    partner_block,
    halo_list,
    grain_cell,
    tile_cell_block,
    pressure_old,
    pressure_source,
    solid_old,
):
    held_grains = grain_count[0]
    slots_here = grain_pos.shape[1]
    tiles_here = slots_here // BLOCK
    live_mask = (jnp.arange(slots_here) < held_grains).astype(jnp.float32)
    grain_state = jnp.concatenate([grain_pos, grain_vel], 0)
    outgoing = jnp.take(grain_state, halo_list.reshape(-1), axis=1)
    rimmed = with_halo(outgoing, (("reg", 1),), HALO)
    extended = jnp.concatenate([grain_state, rimmed[:, :HALO], rimmed[:, 3 * HALO :]], 1)
    contact = contact_forces(grain_state, extended, contact_rows, contact_stiff, partner_block)
    grid_shape = pressure_old.shape
    block_count = pressure_old.size // BLOCK
    inner = (
        grain_cell.reshape(tiles_here, BLOCK)[:, :, None]
        == lax.broadcasted_iota(jnp.int32, (1, 1, BLOCK), 2)
    ).astype(jnp.float32)
    loads = jnp.stack([grain_vol * live_mask, drag_coef * live_mask]).reshape(2, tiles_here, BLOCK)
    tile_loads = jnp.einsum("ltg,tgc->ltc", loads, inner, precision=lax.Precision.HIGHEST)
    part_fields = place_blocks(tile_loads, tile_cell_block, block_count, grid_shape)
    solid_part, drag_part = (part_fields[0], part_fields[1])
    solid_now, drag_sum = lax.psum((solid_part, drag_part), "grp")
    pressure, weight = relax(
        pressure_old, pressure_source, solid_old, solid_now, drag_sum, rim_whole
    )
    padded = with_halo(pressure, (("reg", 0),), 1)
    padded = jnp.pad(padded, ((0, 0), (1, 1), (1, 1)))
    grad_x = 0.5 * (padded[2:, 1:-1, 1:-1] - padded[:-2, 1:-1, 1:-1])
    grad_y = 0.5 * (padded[1:-1, 2:, 1:-1] - padded[1:-1, :-2, 1:-1])
    grad_z = 0.5 * (padded[1:-1, 1:-1, 2:] - padded[1:-1, 1:-1, :-2])
    fields = jnp.stack([grad_x, grad_y, grad_z, weight]).reshape(4, block_count, BLOCK)
    picking = (
        tile_cell_block[:, None] == lax.broadcasted_iota(jnp.int32, (1, block_count), 1)
    ).astype(jnp.float32)
    tile_fields = jnp.einsum("lbc,tb->ltc", fields, picking, precision=lax.Precision.HIGHEST)
    at_grain = jnp.einsum(
        "ltc,tgc->ltg", tile_fields, inner, precision=lax.Precision.HIGHEST
    ).reshape(4, slots_here)
    gradient = at_grain[:3]
    fluid_vel = -gradient * at_grain[3]
    force = contact - grain_vol * gradient + drag_coef * (fluid_vel - grain_vel)
    return (grain_vel + TIME_STEP * force / grain_vol) * live_mask


def solution(mesh):
    in_specs = (
        P(None, ("grp", "reg")),
        P(None, ("grp", "reg")),
        P(("grp", "reg")),
        P(("grp", "reg")),
        P(("grp", "reg")),
        P(None, ("grp", "reg")),
        P(None, ("grp", "reg")),
        P(("grp", "reg")),
        P(None, ("grp", "reg")),
        P(("grp", "reg")),
        P(("grp", "reg")),
        P("reg", None, None),
        P("reg", None, None),
        P("reg", None, None),
    )
    out_specs = P(None, ("grp", "reg"))
    return jax.shard_map(
        on_device, mesh=mesh, in_specs=in_specs, out_specs=out_specs, check_vma=False
    )
```

profile of v0, /device:TPU:32, one launch (start us, length us, event | category | flops | bytes accessed | tf_op | source)
XLA Modules:
  0.0 306.9 jit_solution(5965793484552632646)
XLA Ops:
  6.5 1.1 fusion.122
  7.6 5.4 %collective-permute-start.2 = (f32[1,128,512]{2,1,0:T(8,128)S(1)}, f32[1,128,512]{2,1,0:T(8,128)S(1)}, u32[]{:S(2)}, u32[]{:S(2)}) collective-permute-start(f32[1,128,512]{2,1,0:T(8,128)S(1)} %get-tuple-element.217), channel_id=1, source_target_pairs={{1,0},{2,1},{3,2},{4,3},{5,4},{6,5},{7,6},{8,7},{9,8},{10,9},{11,1... | collective-permute-start | bytes 786440 | tf_op jit(solution)/shard_map/ppermute | solution.py:24
  13.0 1.9 collective-permute-start.3
  16.5 6.5 %fusion.76 = f32[2,128,128]{2,0,1:T(2,128)S(1)} fusion(s32[128,128]{1,0:T(8,128)} %bitcast.111, f32[1,128,128]{2,0,1:T(1,128)S(1)} %bitcast.109, f32[1,128,128]{2,0,1:T(1,128)S(1)} %bitcast.110), kind=kOutput, calls=%fused_computation.122 | convolution fusion | flops 52461568 | bytes 327680 | tf_op jit(solution)/shard_map/ltg,tgc->ltc/dot_general | solution.py:124
  23.0 1.1 convolution_bitcast_fusion.1
  24.3 1.1 squeeze.58
  25.4 1.2 squeeze.59
  27.5 5.3 %copy.24 = f32[6,16384]{0,1:T(8,128)} copy(f32[6,16384]{1,0:T(8,128)S(1)} %get-tuple-element.219) | data formatting | bytes 786432 | tf_op jit(solution)/shard_map/concatenate | solution.py:112
  33.0 31.1 %gather_fusion = f32[8192,6]{1,0:T(8,128)} fusion(f32[6,16384]{0,1:T(8,128)} %copy.24, s32[8192]{0:T(1024)S(1)} %broadcast_clamp_fusion), kind=kCustom, calls=%fused_computation | custom fusion | bytes 425984 | tf_op jit(solution)/shard_map/jit(_take)/gather | solution.py:113
  64.0 6.3 %select_bitcast_fusion = f32[6,8192]{0,1:T(8,128)S(1)} fusion(f32[8192,6]{1,0:T(8,128)} %gather_fusion, pred[8192]{0:T(1024)(128)(4,1)S(1)} %compare_and_fusion), kind=kLoop, calls=%fused_computation.99 | loop fusion | flops 49152 | bytes 401408 | tf_op jit(solution)/shard_map/jit(_take)/select_n | solution.py:113
  70.3 1.6 fusion.116
  71.9 2.9 copy.25
  74.8 2.0 collective-permute-start
  76.8 1.3 copy.26
  78.1 6.9 %collective-permute-start.1 = (f32[6,4096]{1,0:T(8,128)}, f32[6,4096]{1,0:T(8,128)}, u32[]{:S(2)}, u32[]{:S(2)}) collective-permute-start(f32[6,4096]{1,0:T(8,128)} %copy.26), channel_id=1, source_target_pairs={{1,0},{2,1},{3,2},{4,3},{5,4},{6,5},{7,6},{8,7},{9,8},{10,9},{11,1... | collective-permute-start | bytes 294920 | tf_op jit(solution)/shard_map/ppermute | solution.py:24
  85.7 2.0 select_maximum_fusion.8
  88.4 3.9 %fusion.95 = (f32[4,128,512]{2,1,0:T(8,128)S(1)}, f32[4,128,512]{2,1,0:T(8,128)S(1)}) fusion(f32[6,130,514]{2,1,0:T(8,128)S(1)} %select_maximum_fusion.8, f32[4,128,512]{2,1,0:T(8,128)} %param.27, f32[1,128,512]{2,1,0:T(8,128)} %collective-permute-done.3, f32[1,128,512]{2,1,0:T(8,128)} %copy-done.10, f32[4,128,512]{2,1,0:T(8,128)} %get-tuple-element.180, ...), kind=kLoop, calls=%fused_computation.164 | loop fusion | flops 4456448 | bytes 12058624 | tf_op jit(solution)/shard_map/div | solution.py:45
  92.4 7.4 %collective-permute-start.4 = (f32[1,128,512]{2,1,0:T(8,128)S(1)}, f32[1,128,512]{2,1,0:T(8,128)S(1)}, u32[]{:S(2)}, u32[]{:S(2)}) collective-permute-start(f32[1,128,512]{2,1,0:T(8,128)S(1)} %get-tuple-element.215), channel_id=1, source_target_pairs={{1,0},{2,1},{3,2},{4,3},{5,4},{6,5},{7,6},{8,7},{9,8},{10,9},{11,1... | collective-permute-start | bytes 786440 | tf_op jit(solution)/shard_map/ppermute | solution.py:24
  99.8 1.9 collective-permute-start.5
  101.8 4.1 %collective-permute-done.4 = f32[1,128,512]{2,1,0:T(8,128)S(1)} collective-permute-done((f32[1,128,512]{2,1,0:T(8,128)S(1)}, f32[1,128,512]{2,1,0:T(8,128)S(1)}, u32[]{:S(2)}, u32[]{:S(2)}) %collective-permute-start.4) | collective-permute-done | bytes 262176 | tf_op jit(solution)/shard_map/ppermute | solution.py:24
  105.9 7.1 %collective-permute-done.5 = f32[1,128,512]{2,1,0:T(8,128)S(1)} collective-permute-done((f32[1,128,512]{2,1,0:T(8,128)S(1)}, f32[1,128,512]{2,1,0:T(8,128)S(1)}, u32[]{:S(2)}, u32[]{:S(2)}) %collective-permute-start.5) | collective-permute-done | bytes 262176 | tf_op jit(solution)/shard_map/ppermute | solution.py:23
  113.7 1.1 fusion.91
  114.8 1.0 copy-done.2
  116.6 1.9 collective-permute-start.6
  118.5 3.9 %collective-permute-start.7 = (f32[1,128,512]{2,1,0:T(8,128)}, f32[1,128,512]{2,1,0:T(8,128)}, u32[]{:S(2)}, u32[]{:S(2)}) collective-permute-start(f32[1,128,512]{2,1,0:T(8,128)} %get-tuple-element.212), channel_id=1, source_target_pairs={{0,1},{1,2},{2,3},{3,4},{4,5},{5,6},{6,7},{7,8},{8,9},{9,10},{10,1... | collective-permute-start | bytes 786440 | tf_op jit(solution)/shard_map/ppermute | solution.py:23
  124.3 2.1 maximum_bitcast_fusion
  126.4 2.6 gather_fusion.1
  129.0 2.2 collective-permute-done.7
  131.2 2.0 select_maximum_fusion.4
  133.2 2.1 fusion.87
  135.3 3.0 collective-permute-start.8
  138.3 3.2 %collective-permute-start.9 = (f32[1,128,512]{2,1,0:T(8,128)S(1)}, f32[1,128,512]{2,1,0:T(8,128)S(1)}, u32[]{:S(2)}, u32[]{:S(2)}) collective-permute-start(f32[1,128,512]{2,1,0:T(8,128)S(1)} %get-tuple-element.210), channel_id=1, source_target_pairs={{0,1},{1,2},{2,3},{3,4},{4,5},{5,6},{6,7},{7,8},{8,9},{9,10},{10,1... | collective-permute-start | bytes 786440 | tf_op jit(solution)/shard_map/ppermute | solution.py:23
  141.7 1.1 pad_maximum_fusion.10
  142.8 1.1 collective-permute-done.8
  143.9 6.2 %collective-permute-done.9 = f32[1,128,512]{2,1,0:T(8,128)S(1)} collective-permute-done((f32[1,128,512]{2,1,0:T(8,128)S(1)}, f32[1,128,512]{2,1,0:T(8,128)S(1)}, u32[]{:S(2)}, u32[]{:S(2)}) %collective-permute-start.9) | collective-permute-done | bytes 262176 | tf_op jit(solution)/shard_map/ppermute | solution.py:23
  150.7 2.1 fusion.83
  152.8 1.0 copy-done.4
  154.7 1.9 collective-permute-start.10
  156.6 3.9 %collective-permute-start.11 = (f32[1,128,512]{2,1,0:T(8,128)}, f32[1,128,512]{2,1,0:T(8,128)S(1)}, u32[]{:S(2)}, u32[]{:S(2)}) collective-permute-start(f32[1,128,512]{2,1,0:T(8,128)} %get-tuple-element.208), channel_id=1, source_target_pairs={{0,1},{1,2},{2,3},{3,4},{4,5},{5,6},{6,7},{7,8},{8,9},{9,10},{10,1... | collective-permute-start | bytes 786440 | tf_op jit(solution)/shard_map/ppermute | solution.py:23
  160.6 119.8 %while.15 = (s32[]{:T(128)}, f32[3,128,128]{2,0,1:T(4,128)S(1)}, s32[8,128,128]{2,1,0:T(8,128)}, f32[8,128,128]{2,1,0:T(8,128)}, f32[6,128,256]{2,0,1:T(8,128)},...) while((s32[]{:T(128)}, f32[3,128,128]{2,0,1:T(4,128)S(1)}, ...), condition=%wide.region_2.3_spmd.clone.clone, body=%wide.region_0.0_spmd.clone.clone.sunk | while | flops 24945676 | bytes 434535 | solution.py:88
  162.1 4.3 %convolution_bitcast_fusion.3 = f32[6,8,128]{2,0,1:T(8,128)S(1)} fusion(f32[8,128]{1,0:T(8,128)S(1)} %get-tuple-element.269, s32[8,128]{1,0:T(8,128)S(1)} %get-tuple-element.270, f32[8,128]{1,0:T(8,128)S(1)} %get-tuple-element.271, s32[8,128]{1,0:T(8,128)S(1)} %get-tuple-element.272, f32[8,128]{1,0:T(8,128)S(1)} %get-tuple-element.273, ...), kind=kOutput, calls=%fused_computation.11.clone.1 | convolution fusion | flops 24903680 | bytes 155652 | tf_op jit(solution)/shard_map/while/body/eval_jaxpr/tij,ctj->cti/dot_general | solution.py:80
  169.6 4.3 %convolution_bitcast_fusion.3 = f32[6,8,128]{2,0,1:T(8,128)S(1)} fusion(f32[8,128]{1,0:T(8,128)S(1)} %get-tuple-element.269, s32[8,128]{1,0:T(8,128)S(1)} %get-tuple-element.270, f32[8,128]{1,0:T(8,128)S(1)} %get-tuple-element.271, s32[8,128]{1,0:T(8,128)S(1)} %get-tuple-element.272, f32[8,128]{1,0:T(8,128)S(1)} %get-tuple-element.273, ...), kind=kOutput, calls=%fused_computation.11.clone.1 | convolution fusion | flops 24903680 | bytes 155652 | tf_op jit(solution)/shard_map/while/body/eval_jaxpr/tij,ctj->cti/dot_general | solution.py:80
  177.1 4.3 %convolution_bitcast_fusion.3 = f32[6,8,128]{2,0,1:T(8,128)S(1)} fusion(f32[8,128]{1,0:T(8,128)S(1)} %get-tuple-element.269, s32[8,128]{1,0:T(8,128)S(1)} %get-tuple-element.270, f32[8,128]{1,0:T(8,128)S(1)} %get-tuple-element.271, s32[8,128]{1,0:T(8,128)S(1)} %get-tuple-element.272, f32[8,128]{1,0:T(8,128)S(1)} %get-tuple-element.273, ...), kind=kOutput, calls=%fused_computation.11.clone.1 | convolution fusion | flops 24903680 | bytes 155652 | tf_op jit(solution)/shard_map/while/body/eval_jaxpr/tij,ctj->cti/dot_general | solution.py:80
  184.6 4.3 %convolution_bitcast_fusion.3 = f32[6,8,128]{2,0,1:T(8,128)S(1)} fusion(f32[8,128]{1,0:T(8,128)S(1)} %get-tuple-element.269, s32[8,128]{1,0:T(8,128)S(1)} %get-tuple-element.270, f32[8,128]{1,0:T(8,128)S(1)} %get-tuple-element.271, s32[8,128]{1,0:T(8,128)S(1)} %get-tuple-element.272, f32[8,128]{1,0:T(8,128)S(1)} %get-tuple-element.273, ...), kind=kOutput, calls=%fused_computation.11.clone.1 | convolution fusion | flops 24903680 | bytes 155652 | tf_op jit(solution)/shard_map/while/body/eval_jaxpr/tij,ctj->cti/dot_general | solution.py:80
  192.1 4.3 %convolution_bitcast_fusion.3 = f32[6,8,128]{2,0,1:T(8,128)S(1)} fusion(f32[8,128]{1,0:T(8,128)S(1)} %get-tuple-element.269, s32[8,128]{1,0:T(8,128)S(1)} %get-tuple-element.270, f32[8,128]{1,0:T(8,128)S(1)} %get-tuple-element.271, s32[8,128]{1,0:T(8,128)S(1)} %get-tuple-element.272, f32[8,128]{1,0:T(8,128)S(1)} %get-tuple-element.273, ...), kind=kOutput, calls=%fused_computation.11.clone.1 | convolution fusion | flops 24903680 | bytes 155652 | tf_op jit(solution)/shard_map/while/body/eval_jaxpr/tij,ctj->cti/dot_general | solution.py:80
  199.6 4.3 %convolution_bitcast_fusion.3 = f32[6,8,128]{2,0,1:T(8,128)S(1)} fusion(f32[8,128]{1,0:T(8,128)S(1)} %get-tuple-element.269, s32[8,128]{1,0:T(8,128)S(1)} %get-tuple-element.270, f32[8,128]{1,0:T(8,128)S(1)} %get-tuple-element.271, s32[8,128]{1,0:T(8,128)S(1)} %get-tuple-element.272, f32[8,128]{1,0:T(8,128)S(1)} %get-tuple-element.273, ...), kind=kOutput, calls=%fused_computation.11.clone.1 | convolution fusion | flops 24903680 | bytes 155652 | tf_op jit(solution)/shard_map/while/body/eval_jaxpr/tij,ctj->cti/dot_general | solution.py:80
  207.1 4.3 %convolution_bitcast_fusion.3 = f32[6,8,128]{2,0,1:T(8,128)S(1)} fusion(f32[8,128]{1,0:T(8,128)S(1)} %get-tuple-element.269, s32[8,128]{1,0:T(8,128)S(1)} %get-tuple-element.270, f32[8,128]{1,0:T(8,128)S(1)} %get-tuple-element.271, s32[8,128]{1,0:T(8,128)S(1)} %get-tuple-element.272, f32[8,128]{1,0:T(8,128)S(1)} %get-tuple-element.273, ...), kind=kOutput, calls=%fused_computation.11.clone.1 | convolution fusion | flops 24903680 | bytes 155652 | tf_op jit(solution)/shard_map/while/body/eval_jaxpr/tij,ctj->cti/dot_general | solution.py:80
  214.6 4.3 %convolution_bitcast_fusion.3 = f32[6,8,128]{2,0,1:T(8,128)S(1)} fusion(f32[8,128]{1,0:T(8,128)S(1)} %get-tuple-element.269, s32[8,128]{1,0:T(8,128)S(1)} %get-tuple-element.270, f32[8,128]{1,0:T(8,128)S(1)} %get-tuple-element.271, s32[8,128]{1,0:T(8,128)S(1)} %get-tuple-element.272, f32[8,128]{1,0:T(8,128)S(1)} %get-tuple-element.273, ...), kind=kOutput, calls=%fused_computation.11.clone.1 | convolution fusion | flops 24903680 | bytes 155652 | tf_op jit(solution)/shard_map/while/body/eval_jaxpr/tij,ctj->cti/dot_general | solution.py:80
  222.0 4.3 %convolution_bitcast_fusion.3 = f32[6,8,128]{2,0,1:T(8,128)S(1)} fusion(f32[8,128]{1,0:T(8,128)S(1)} %get-tuple-element.269, s32[8,128]{1,0:T(8,128)S(1)} %get-tuple-element.270, f32[8,128]{1,0:T(8,128)S(1)} %get-tuple-element.271, s32[8,128]{1,0:T(8,128)S(1)} %get-tuple-element.272, f32[8,128]{1,0:T(8,128)S(1)} %get-tuple-element.273, ...), kind=kOutput, calls=%fused_computation.11.clone.1 | convolution fusion | flops 24903680 | bytes 155652 | tf_op jit(solution)/shard_map/while/body/eval_jaxpr/tij,ctj->cti/dot_general | solution.py:80
  229.5 4.3 %convolution_bitcast_fusion.3 = f32[6,8,128]{2,0,1:T(8,128)S(1)} fusion(f32[8,128]{1,0:T(8,128)S(1)} %get-tuple-element.269, s32[8,128]{1,0:T(8,128)S(1)} %get-tuple-element.270, f32[8,128]{1,0:T(8,128)S(1)} %get-tuple-element.271, s32[8,128]{1,0:T(8,128)S(1)} %get-tuple-element.272, f32[8,128]{1,0:T(8,128)S(1)} %get-tuple-element.273, ...), kind=kOutput, calls=%fused_computation.11.clone.1 | convolution fusion | flops 24903680 | bytes 155652 | tf_op jit(solution)/shard_map/while/body/eval_jaxpr/tij,ctj->cti/dot_general | solution.py:80
  237.0 4.3 %convolution_bitcast_fusion.3 = f32[6,8,128]{2,0,1:T(8,128)S(1)} fusion(f32[8,128]{1,0:T(8,128)S(1)} %get-tuple-element.269, s32[8,128]{1,0:T(8,128)S(1)} %get-tuple-element.270, f32[8,128]{1,0:T(8,128)S(1)} %get-tuple-element.271, s32[8,128]{1,0:T(8,128)S(1)} %get-tuple-element.272, f32[8,128]{1,0:T(8,128)S(1)} %get-tuple-element.273, ...), kind=kOutput, calls=%fused_computation.11.clone.1 | convolution fusion | flops 24903680 | bytes 155652 | tf_op jit(solution)/shard_map/while/body/eval_jaxpr/tij,ctj->cti/dot_general | solution.py:80
  244.5 4.3 %convolution_bitcast_fusion.3 = f32[6,8,128]{2,0,1:T(8,128)S(1)} fusion(f32[8,128]{1,0:T(8,128)S(1)} %get-tuple-element.269, s32[8,128]{1,0:T(8,128)S(1)} %get-tuple-element.270, f32[8,128]{1,0:T(8,128)S(1)} %get-tuple-element.271, s32[8,128]{1,0:T(8,128)S(1)} %get-tuple-element.272, f32[8,128]{1,0:T(8,128)S(1)} %get-tuple-element.273, ...), kind=kOutput, calls=%fused_computation.11.clone.1 | convolution fusion | flops 24903680 | bytes 155652 | tf_op jit(solution)/shard_map/while/body/eval_jaxpr/tij,ctj->cti/dot_general | solution.py:80
  252.0 4.3 %convolution_bitcast_fusion.3 = f32[6,8,128]{2,0,1:T(8,128)S(1)} fusion(f32[8,128]{1,0:T(8,128)S(1)} %get-tuple-element.269, s32[8,128]{1,0:T(8,128)S(1)} %get-tuple-element.270, f32[8,128]{1,0:T(8,128)S(1)} %get-tuple-element.271, s32[8,128]{1,0:T(8,128)S(1)} %get-tuple-element.272, f32[8,128]{1,0:T(8,128)S(1)} %get-tuple-element.273, ...), kind=kOutput, calls=%fused_computation.11.clone.1 | convolution fusion | flops 24903680 | bytes 155652 | tf_op jit(solution)/shard_map/while/body/eval_jaxpr/tij,ctj->cti/dot_general | solution.py:80
  259.5 4.3 %convolution_bitcast_fusion.3 = f32[6,8,128]{2,0,1:T(8,128)S(1)} fusion(f32[8,128]{1,0:T(8,128)S(1)} %get-tuple-element.269, s32[8,128]{1,0:T(8,128)S(1)} %get-tuple-element.270, f32[8,128]{1,0:T(8,128)S(1)} %get-tuple-element.271, s32[8,128]{1,0:T(8,128)S(1)} %get-tuple-element.272, f32[8,128]{1,0:T(8,128)S(1)} %get-tuple-element.273, ...), kind=kOutput, calls=%fused_computation.11.clone.1 | convolution fusion | flops 24903680 | bytes 155652 | tf_op jit(solution)/shard_map/while/body/eval_jaxpr/tij,ctj->cti/dot_general | solution.py:80
  266.9 4.3 %convolution_bitcast_fusion.3 = f32[6,8,128]{2,0,1:T(8,128)S(1)} fusion(f32[8,128]{1,0:T(8,128)S(1)} %get-tuple-element.269, s32[8,128]{1,0:T(8,128)S(1)} %get-tuple-element.270, f32[8,128]{1,0:T(8,128)S(1)} %get-tuple-element.271, s32[8,128]{1,0:T(8,128)S(1)} %get-tuple-element.272, f32[8,128]{1,0:T(8,128)S(1)} %get-tuple-element.273, ...), kind=kOutput, calls=%fused_computation.11.clone.1 | convolution fusion | flops 24903680 | bytes 155652 | tf_op jit(solution)/shard_map/while/body/eval_jaxpr/tij,ctj->cti/dot_general | solution.py:80
  274.4 4.3 %convolution_bitcast_fusion.3 = f32[6,8,128]{2,0,1:T(8,128)S(1)} fusion(f32[8,128]{1,0:T(8,128)S(1)} %get-tuple-element.269, s32[8,128]{1,0:T(8,128)S(1)} %get-tuple-element.270, f32[8,128]{1,0:T(8,128)S(1)} %get-tuple-element.271, s32[8,128]{1,0:T(8,128)S(1)} %get-tuple-element.272, f32[8,128]{1,0:T(8,128)S(1)} %get-tuple-element.273, ...), kind=kOutput, calls=%fused_computation.11.clone.1 | convolution fusion | flops 24903680 | bytes 155652 | tf_op jit(solution)/shard_map/while/body/eval_jaxpr/tij,ctj->cti/dot_general | solution.py:80
  280.4 1.1 stack.30
  282.2 1.0 stack.27
  283.9 0.9 fusion.78
  284.9 1.0 stack.28
  285.9 1.1 stack.29
  287.5 3.5 %fusion.73 = f32[4,128,128]{2,1,0:T(8,128)S(1)} fusion(f32[1,2048,128]{2,1,0:T(8,128)S(1)} %copy-done.11, f32[1,2048,128]{2,1,0:T(8,128)} %stack.29, f32[1,2048,128]{2,1,0:T(8,128)} %stack.28, f32[1,2048,128]{2,1,0:T(8,128)} %stack.27, s32[128]{0:T(128)S(1)} %copy-done.18), kind=kOutput, calls=%fused_computation.121 | convolution fusion | flops 1614020608 | bytes 4456960 | tf_op jit(solution)/shard_map/lbc,tb->ltc/dot_general | solution.py:140
  291.0 8.0 %fusion.72 = f32[4,128,128]{2,0,1:T(4,128)S(1)} fusion(s32[128,128]{1,0:T(8,128)S(1)} %bitcast.112, f32[4,128,128]{2,1,0:T(8,128)S(1)} %fusion.73), kind=kOutput, calls=%fused_computation.120 | convolution fusion | flops 102760448 | bytes 589824 | tf_op jit(solution)/shard_map/ltc,tgc->ltg/dot_general | solution.py:141
  299.2 0.9 fusion.105
  (139 shorter events, 61.2 us)
Async XLA Ops:
  6.5 81.9 %all-reduce.8.cloned.1.call-start = ((), (), s32[]{:S(2)}) async-start(), calls=%async_computation | async-start | bytes 4194304 | tf_op jit(solution)/shard_map/psum | solution.py:127
  7.6 77.4 %collective-permute-start.2 = (f32[1,128,512]{2,1,0:T(8,128)S(1)}, f32[1,128,512]{2,1,0:T(8,128)S(1)}, u32[]{:S(2)}, u32[]{:S(2)}) collective-permute-start(f32[1,128,512]{2,1,0:T(8,128)S(1)} %get-tuple-element.217), channel_id=1, source_target_pairs={{1,0},{2,1},{3,2},{4,3},{5,4},{6,5},{7,6},{8,7},{9,8},{10,9},{11,1... | collective-permute-start | bytes 786440 | tf_op jit(solution)/shard_map/ppermute | solution.py:24
  13.0 72.7 %collective-permute-start.3 = (f32[1,128,512]{2,1,0:T(8,128)S(1)}, f32[1,128,512]{2,1,0:T(8,128)}, u32[]{:S(2)}, u32[]{:S(2)}) collective-permute-start(f32[1,128,512]{2,1,0:T(8,128)S(1)} %get-tuple-element.216), channel_id=1, source_target_pairs={{0,1},{1,2},{2,3},{3,4},{4,5},{5,6},{6,7},{7,8},{8,9},{9,10},{10,1... | collective-permute-start | bytes 786440 | tf_op jit(solution)/shard_map/ppermute | solution.py:23
  16.5 6.5 %copy-start.18 = (s32[128]{0:T(128)S(1)}, s32[128]{0:T(128)}, u32[]{:S(2)}) copy-start(s32[128]{0:T(128)} %param.26) | copy-start | bytes 1540
  25.4 1.2 copy-start.7
  25.4 1.2 copy-start.12
  27.5 5.3 %copy-start.17 = (s32[2,4096]{1,0:T(2,128)S(1)}, s32[2,4096]{1,0:T(2,128)}, u32[]{:S(2)}) copy-start(s32[2,4096]{1,0:T(2,128)} %param.24) | copy-start | bytes 98308
  74.8 49.5 %collective-permute-start = (f32[6,4096]{1,0:T(8,128)}, f32[6,4096]{1,0:T(8,128)}, u32[]{:S(2)}, u32[]{:S(2)}) collective-permute-start(f32[6,4096]{1,0:T(8,128)} %copy.25), channel_id=1, source_target_pairs={{0,1},{1,2},{2,3},{3,4},{4,5},{5,6},{6,7},{7,8},{8,9},{9,10},{10,1... | collective-permute-start | bytes 294920 | tf_op jit(solution)/shard_map/ppermute | solution.py:23
  78.1 46.2 %collective-permute-start.1 = (f32[6,4096]{1,0:T(8,128)}, f32[6,4096]{1,0:T(8,128)}, u32[]{:S(2)}, u32[]{:S(2)}) collective-permute-start(f32[6,4096]{1,0:T(8,128)} %copy.26), channel_id=1, source_target_pairs={{1,0},{2,1},{3,2},{4,3},{5,4},{6,5},{7,6},{8,7},{9,8},{10,9},{11,1... | collective-permute-start | bytes 294920 | tf_op jit(solution)/shard_map/ppermute | solution.py:24
  85.0 0.7 copy-start.10
  88.4 13.3 %copy-start.20 = (s32[128]{0:T(128)S(1)}, s32[128]{0:T(128)}, u32[]{:S(2)}) copy-start(s32[128]{0:T(128)} %param.23) | copy-start | bytes 1540
  92.4 21.3 %copy-start = (f32[4,128,512]{2,1,0:T(8,128)S(1)}, f32[4,128,512]{2,1,0:T(8,128)}, u32[]{:S(2)}) copy-start(f32[4,128,512]{2,1,0:T(8,128)} %get-tuple-element.180) | copy-start | bytes 3145732
  92.4 21.3 %copy-start.1 = (f32[4,128,512]{2,1,0:T(8,128)S(1)}, f32[4,128,512]{2,1,0:T(8,128)}, u32[]{:S(2)}) copy-start(f32[4,128,512]{2,1,0:T(8,128)} %get-tuple-element.181) | copy-start | bytes 3145732
  92.4 13.4 %collective-permute-start.4 = (f32[1,128,512]{2,1,0:T(8,128)S(1)}, f32[1,128,512]{2,1,0:T(8,128)S(1)}, u32[]{:S(2)}, u32[]{:S(2)}) collective-permute-start(f32[1,128,512]{2,1,0:T(8,128)S(1)} %get-tuple-element.215), channel_id=1, source_target_pairs={{1,0},{2,1},{3,2},{4,3},{5,4},{6,5},{7,6},{8,7},{9,8},{10,9},{11,1... | collective-permute-start | bytes 786440 | tf_op jit(solution)/shard_map/ppermute | solution.py:24
  99.8 13.2 %collective-permute-start.5 = (f32[1,128,512]{2,1,0:T(8,128)S(1)}, f32[1,128,512]{2,1,0:T(8,128)S(1)}, u32[]{:S(2)}, u32[]{:S(2)}) collective-permute-start(f32[1,128,512]{2,1,0:T(8,128)S(1)} %get-tuple-element.214), channel_id=1, source_target_pairs={{0,1},{1,2},{2,3},{3,4},{4,5},{5,6},{6,7},{7,8},{8,9},{9,10},{10,1... | collective-permute-start | bytes 786440 | tf_op jit(solution)/shard_map/ppermute | solution.py:23
  113.7 8.8 %copy-start.13 = (f32[8,16384]{1,0:T(8,128)S(1)}, f32[8,16384]{1,0:T(8,128)}, u32[]{:S(2)}) copy-start(f32[8,16384]{1,0:T(8,128)} %param.22) | copy-start | bytes 1572868
  114.8 1.0 copy-start.2
  115.8 7.6 %copy-start.14 = (s32[8,16384]{1,0:T(8,128)S(1)}, s32[8,16384]{1,0:T(8,128)}, u32[]{:S(2)}) copy-start(s32[8,16384]{1,0:T(8,128)} %param.21) | copy-start | bytes 1572868
  116.6 12.4 %collective-permute-start.6 = (f32[1,128,512]{2,1,0:T(8,128)}, f32[1,128,512]{2,1,0:T(8,128)}, u32[]{:S(2)}, u32[]{:S(2)}) collective-permute-start(f32[1,128,512]{2,1,0:T(8,128)} %get-tuple-element.213), channel_id=1, source_target_pairs={{1,0},{2,1},{3,2},{4,3},{5,4},{6,5},{7,6},{8,7},{9,8},{10,9},{11,1... | collective-permute-start | bytes 786440 | tf_op jit(solution)/shard_map/ppermute | solution.py:24
  118.5 12.6 %collective-permute-start.7 = (f32[1,128,512]{2,1,0:T(8,128)}, f32[1,128,512]{2,1,0:T(8,128)}, u32[]{:S(2)}, u32[]{:S(2)}) collective-permute-start(f32[1,128,512]{2,1,0:T(8,128)} %get-tuple-element.212), channel_id=1, source_target_pairs={{0,1},{1,2},{2,3},{3,4},{4,5},{5,6},{6,7},{7,8},{8,9},{9,10},{10,1... | collective-permute-start | bytes 786440 | tf_op jit(solution)/shard_map/ppermute | solution.py:23
  129.0 4.2 %copy-start.3 = (f32[4,128,512]{2,1,0:T(8,128)S(1)}, f32[4,128,512]{2,1,0:T(8,128)}, u32[]{:S(2)}) copy-start(f32[4,128,512]{2,1,0:T(8,128)} %copy-done.2) | copy-start | bytes 3145732
  133.2 8.3 %copy-start.9 = (f32[128,6,128]{2,1,0:T(8,128)S(1)}, f32[128,6,128]{2,1,0:T(8,128)}, u32[]{:S(2)}) copy-start(f32[128,6,128]{2,1,0:T(8,128)} %gather_fusion.1) | copy-start | bytes 1179652
  135.3 6.4 %copy-start.8 = (f32[6,128,128]{2,0,1:T(8,128)S(1)}, f32[6,128,128]{2,0,1:T(8,128)}, u32[]{:S(2)}) copy-start(f32[6,128,128]{2,0,1:T(8,128)} %get-tuple-element.218) | copy-start | bytes 1179652
  135.3 8.6 %collective-permute-start.8 = (f32[1,128,512]{2,1,0:T(8,128)S(1)}, f32[1,128,512]{2,1,0:T(8,128)S(1)}, u32[]{:S(2)}, u32[]{:S(2)}) collective-permute-start(f32[1,128,512]{2,1,0:T(8,128)S(1)} %get-tuple-element.211), channel_id=1, source_target_pairs={{1,0},{2,1},{3,2},{4,3},{5,4},{6,5},{7,6},{8,7},{9,8},{10,9},{11,1... | collective-permute-start | bytes 786440 | tf_op jit(solution)/shard_map/ppermute | solution.py:24
  138.3 11.7 %collective-permute-start.9 = (f32[1,128,512]{2,1,0:T(8,128)S(1)}, f32[1,128,512]{2,1,0:T(8,128)S(1)}, u32[]{:S(2)}, u32[]{:S(2)}) collective-permute-start(f32[1,128,512]{2,1,0:T(8,128)S(1)} %get-tuple-element.210), channel_id=1, source_target_pairs={{0,1},{1,2},{2,3},{3,4},{4,5},{5,6},{6,7},{7,8},{8,9},{9,10},{10,1... | collective-permute-start | bytes 786440 | tf_op jit(solution)/shard_map/ppermute | solution.py:23
  152.8 1.0 copy-start.4
  154.7 126.8 %collective-permute-start.10 = (f32[1,128,512]{2,1,0:T(8,128)}, f32[1,128,512]{2,1,0:T(8,128)S(1)}, u32[]{:S(2)}, u32[]{:S(2)}) collective-permute-start(f32[1,128,512]{2,1,0:T(8,128)} %get-tuple-element.209), channel_id=1, source_target_pairs={{1,0},{2,1},{3,2},{4,3},{5,4},{6,5},{7,6},{8,7},{9,8},{10,9},{11,1... | collective-permute-start | bytes 786440 | tf_op jit(solution)/shard_map/ppermute | solution.py:24
  156.6 124.9 %collective-permute-start.11 = (f32[1,128,512]{2,1,0:T(8,128)}, f32[1,128,512]{2,1,0:T(8,128)S(1)}, u32[]{:S(2)}, u32[]{:S(2)}) collective-permute-start(f32[1,128,512]{2,1,0:T(8,128)} %get-tuple-element.208), channel_id=1, source_target_pairs={{0,1},{1,2},{2,3},{3,4},{4,5},{5,6},{6,7},{7,8},{8,9},{9,10},{10,1... | collective-permute-start | bytes 786440 | tf_op jit(solution)/shard_map/ppermute | solution.py:23
  160.6 119.9 %copy-start.6 = (f32[4,128,512]{2,1,0:T(8,128)S(1)}, f32[4,128,512]{2,1,0:T(8,128)}, u32[]{:S(2)}) copy-start(f32[4,128,512]{2,1,0:T(8,128)} %get-tuple-element.203) | copy-start | bytes 3145732
  280.4 1.6 copy-start.5
  285.9 1.6 copy-start.11
  287.5 3.5 %copy-start.19 = (s32[16384]{0:T(1024)S(1)}, s32[16384]{0:T(1024)}, u32[]{:S(2)}) copy-start(s32[16384]{0:T(1024)} %param.25) | copy-start | bytes 196612
  291.0 8.1 %copy-start.15 = (f32[16384]{0:T(1024)S(1)}, f32[16384]{0:T(1024)}, u32[]{:S(2)}) copy-start(f32[16384]{0:T(1024)} %param.19) | copy-start | bytes 196612
  291.0 8.1 %copy-start.16 = (f32[16384]{0:T(1024)S(1)}, f32[16384]{0:T(1024)}, u32[]{:S(2)}) copy-start(f32[16384]{0:T(1024)} %param.18) | copy-start | bytes 196612
Sparse Core Ops, SparseCore 0:
  26.7 61.6 all-reduce.7
where the time goes:
time: 312 us; the launch traced here: 307 us
  matrix products  88.1 us (28%)
  local copies, waits for them, and re-layouts  83.6 us (27%)
  other arithmetic  55.6 us (18%)
  starting transfers between devices  43.3 us (14%)
  waiting for transfers between devices  21.4 us (7%)
  between operations  14.6 us (5%)
    dot_general x16, matrix products, step_forces(): jnp.einsum('tij,ctj->cti', weights, pair_step, precision=lax.Precision.HI...  69 us
    gather x1, local copies, waits for them, and re-layouts, on_device(): outgoing = jnp.take(grain_state, halo_list.reshape(-1), axis=1)  31.1 us
    ppermute x6, starting transfers between devices, with_halo(): after = lax.ppermute(initial, axis, down)  26.5 us
    ppermute x6, starting transfers between devices, with_halo(): before = lax.ppermute(last, axis, up)  16.8 us
    ppermute x6, waiting for transfers between devices, with_halo(): before = lax.ppermute(last, axis, up)  15.5 us
    dynamic_update_slice x16, other arithmetic, step_forces(): lax.dynamic_update_slice_in_dim(forces, spring + damper, first_tile, 1)  13.7 us
    reduce_sum x16, other arithmetic, step_forces(): stiff_total = jnp.sum(jnp.where(rows_step >= 0, stiff_step, 0.0), 0)  13.1 us
    broadcast_in_dim x16, local copies, waits for them, and re-layouts, step_forces(): jnp.where(rows_step[slot_index][:, :, None] == columns, stiff_step[slot_i...  12 us
  transfers between devices with their start and end apart: 13, of which 6 were waited for; matrix products, arithmetic and copies ran while one was open for 64% of the time, Pallas kernels for 0%

commit v1 on v0

v1 whole, which is shorter than its diff:
```python
import functools

import jax
import jax.numpy as jnp
from jax import lax
from jax.experimental import pallas as pl
from jax.experimental.pallas import tpu as pltpu
from jax.sharding import PartitionSpec as P

BLOCK = 128
ITERS = 4
SPRING = 1.0
DAMPING = 0.5
TIME_STEP = 0.5
GHOST = 8
PAD = 8
MESH = pl.DeviceIdType.MESH
F32 = jnp.float32
BF16 = jnp.bfloat16


def iota(shape, axis):
    return lax.broadcasted_iota(jnp.int32, shape, axis)


def split(values):
    high = values.astype(BF16)
    return high, (values - high.astype(F32)).astype(BF16)


def lanes_at(table, lane):
    return jnp.take_along_axis(table, lane, axis=1, mode="promise_in_bounds")


def kernel(
    count_s, partner_s, tile_s, tile_v, pos, vel, vol, drag, cell, rows, stiff, halo, p_old, source, solid_old,
    out,
    loads, ids_all, ids_sib, state, velocity, halo_row, halo_out, contact, pbuf, hbuf, src_v, old_v, coef_a, coef_b,
    fields, part_own, part_sent, part_got, send, recv, local,
):
    tiles, slot_count = vol.shape[0], rows.shape[0]
    planes, width_y, width_z = p_old.shape
    half = width_y // 2
    slab = half + GHOST
    per_row = width_z // BLOCK
    halo_blocks = halo.shape[1] // BLOCK
    group, region = lax.axis_index("grp"), lax.axis_index("reg")
    regions = lax.axis_size("reg")
    core = lax.rem(group, 2)
    sibling = {"grp": group + 1 - 2 * core}
    across = {"grp": lax.rem(group + 2, 4)}
    upper = {"reg": lax.rem(region + 1, regions)}
    lower = {"reg": lax.rem(region + regions - 1, regions)}
    first_y = pl.multiple_of(core * (half - GHOST), 8)
    count = count_s[0]

    def remote(index, src, dst, device):
        return pltpu.make_async_remote_copy(
            src_ref=src, dst_ref=dst, send_sem=send.at[index], recv_sem=recv.at[index],
            device_id=device, device_id_type=MESH,
        )

    barrier = pltpu.get_barrier_semaphore()
    for device in (sibling, across, upper, lower):
        pl.semaphore_signal(barrier, inc=1, device_id=device, device_id_type=MESH)

    inner = pl.ds(PAD, slab)
    rows_y = pl.ds(first_y, slab)
    load_p = pltpu.make_async_copy(p_old.at[:, rows_y, :], pbuf.at[0, :, inner, :], local.at[0])
    load_src = pltpu.make_async_copy(source.at[:, rows_y, :], src_v, local.at[1])
    load_old = pltpu.make_async_copy(solid_old.at[:, rows_y, :], old_v, local.at[2])
    load_p.start()
    load_src.start()
    load_old.start()

    cells = iota((BLOCK, BLOCK), 0)

    def deposit(step, carry):
        first = pl.multiple_of(step * 8, 8)
        cell8 = cell[pl.ds(first, 8), :]
        slot = first * BLOCK + iota((8, BLOCK), 0) * BLOCK + iota((8, BLOCK), 1)
        live = slot < count
        vol8 = jnp.where(live, vol[pl.ds(first, 8), :], 0.0)
        drag8 = jnp.where(live, drag[pl.ds(first, 8), :], 0.0)
        both = jnp.concatenate([vol8, drag8], 0)
        high, low = split(both)
        pieces = jnp.concatenate([high, low], 0)
        total = jnp.zeros((32, BLOCK), F32)
        for tile in range(8):
            hot = (cell8[tile : tile + 1, :] == cells).astype(F32).astype(BF16)
            found = lax.dot_general(pieces, hot, (((1,), (1,)), ((), ())), preferred_element_type=F32)
            total = jnp.where(iota((32, BLOCK), 0) % 8 == tile, found, total)
        total = total[:16] + total[16:]
        loads[0, pl.ds(first, 8), 0:BLOCK] = total[:8]
        loads[0, pl.ds(first, 8), BLOCK : 2 * BLOCK] = total[8:]
        return carry

    lax.fori_loop(0, tiles // 8, deposit, 0)
    ids_all[0] = tile_v[...]
    pl.semaphore_wait(barrier, 4)

    to_sibling = remote(0, loads.at[0], loads.at[1], sibling)
    to_across = remote(1, loads.at[0], loads.at[2], across)
    passed_on = remote(2, loads.at[2], loads.at[3], sibling)
    id_sibling = remote(3, tile_v, ids_all.at[1], sibling)
    id_across = remote(4, tile_v, ids_all.at[2], across)
    id_passed = remote(5, ids_all.at[2], ids_all.at[3], sibling)
    id_across.start()
    to_across.start()
    id_sibling.start()
    to_sibling.start()

    def planes_out(sweep):
        if sweep == 0:
            low, high = p_old.at[0, rows_y, :], p_old.at[planes - 1, rows_y, :]
        else:
            low, high = pbuf.at[sweep, 0, inner, :], pbuf.at[sweep, planes - 1, inner, :]
        return (
            remote(6 + 2 * sweep, low, hbuf.at[sweep, 1], lower),
            remote(7 + 2 * sweep, high, hbuf.at[sweep, 0], upper),
        )

    exchanges = [planes_out(sweep) for sweep in range(ITERS + 1)]
    for copy in exchanges[0]:
        copy.start()

    def tabulate(tile, carry):
        at = pl.ds(pl.multiple_of(tile * BLOCK, BLOCK), BLOCK)
        moved = vel[:, at]
        mixed = SPRING * pos[:, at] - DAMPING * moved
        for part in range(3):
            state[part, pl.ds(tile, 1), :] = mixed[part : part + 1]
            velocity[part, pl.ds(tile, 1), :] = moved[part : part + 1]
        return carry

    lax.fori_loop(0, tiles, tabulate, 0)

    def halo_rows(block, carry):
        at = pl.ds(pl.multiple_of(block * BLOCK, BLOCK), BLOCK)
        for side in range(2):
            halo_row[pl.ds(block + side * halo_blocks, 1), :] = halo[side : side + 1, at]
        return carry

    lax.fori_loop(0, halo_blocks, halo_rows, 0)
    wanted = halo_row[...]
    wanted_row, wanted_lane = wanted >> 7, wanted & (BLOCK - 1)

    def pick(row, picked):
        here = wanted_row == row
        return tuple(
            jnp.where(
                here,
                lanes_at(jnp.broadcast_to(state[part, pl.ds(row, 1), :], wanted.shape), wanted_lane),
                picked[part],
            )
            for part in range(3)
        )

    picked = lax.fori_loop(0, tiles, pick, tuple(jnp.zeros(wanted.shape, F32) for _ in range(3)))
    for part in range(3):
        for side in range(2):
            halo_out[side, part] = picked[part][side * halo_blocks : (side + 1) * halo_blocks]
    w_down = remote(16, halo_out.at[0], state.at[:, pl.ds(tiles + halo_blocks, halo_blocks), :], lower)
    w_up = remote(17, halo_out.at[1], state.at[:, pl.ds(tiles, halo_blocks), :], upper)
    w_down.start()
    w_up.start()

    id_across.wait_recv()
    id_passed.start()
    to_across.wait_recv()
    passed_on.start()

    for sweep in range(ITERS + 1):
        for plane in range(planes):
            pbuf[sweep, plane, 0:PAD, :] = jnp.zeros((PAD, width_z), F32)
            pbuf[sweep, plane, PAD + slab : 2 * PAD + slab, :] = jnp.zeros((PAD, width_z), F32)

    id_sibling.wait_recv()
    keep_ids = pltpu.make_async_copy(ids_all.at[1], ids_sib, local.at[3])
    keep_ids.start()
    id_passed.wait_recv()
    to_sibling.wait_recv()
    passed_on.wait_recv()
    load_p.wait()
    load_src.wait()
    load_old.wait()

    every = loads[...].reshape(4 * tiles, 2 * BLOCK)
    high, low = split(every)
    both = jnp.concatenate([high, low], 1)
    ids = jnp.concatenate([ids_all[source_id] for source_id in range(4)], 1)
    block_of = (iota((slab, 4 * tiles), 0) + first_y) * per_row
    for plane in range(planes):
        hot = jnp.concatenate(
            [
                (block_of + (plane * width_y * per_row + part) == ids).astype(F32).astype(BF16)
                for part in range(per_row)
            ],
            0,
        )
        placed = jnp.dot(hot, both, preferred_element_type=F32)
        placed = placed[:, : 2 * BLOCK] + placed[:, 2 * BLOCK :]
        for part in range(per_row):
            at = slice(part * BLOCK, (part + 1) * BLOCK)
            solid = placed[part * slab : (part + 1) * slab, :BLOCK]
            dragged = placed[part * slab : (part + 1) * slab, BLOCK:]
            porous = 1.0 / (1.0 + solid)
            inverse = 1.0 / (6.0 * porous + dragged + 1.0)
            driving = src_v[plane, :, at] + solid - old_v[plane, :, at]
            coef_a[plane, :, at] = driving * inverse
            coef_b[plane, :, at] = porous * inverse
            fields[(3 * planes + plane) * per_row + part] = 1.0 / (porous + dragged)

    lane = iota((slab, width_z), 1)

    def before_z(values):
        return jnp.where(lane == 0, 0.0, pltpu.roll(values, 1, 1))

    def after_z(values):
        return jnp.where(lane == width_z - 1, 0.0, pltpu.roll(values, width_z - 1, 1))

    def below(sweep, plane):
        if plane == 0:
            return jnp.where(region > 0, hbuf[sweep, 0], 0.0)
        return pbuf[sweep, plane - 1, PAD : PAD + slab, :]

    def above(sweep, plane):
        if plane == planes - 1:
            return jnp.where(region < regions - 1, hbuf[sweep, 1], 0.0)
        return pbuf[sweep, plane + 1, PAD : PAD + slab, :]

    def relax(sweep, plane):
        here = pbuf[sweep - 1, plane, PAD : PAD + slab, :]
        total = below(sweep - 1, plane) + above(sweep - 1, plane)
        total = total + pbuf[sweep - 1, plane, PAD - 1 : PAD + slab - 1, :]
        total = total + pbuf[sweep - 1, plane, PAD + 1 : PAD + slab + 1, :]
        total = total + before_z(here) + after_z(here)
        pbuf[sweep, plane, PAD : PAD + slab, :] = coef_a[plane] + coef_b[plane] * total

    def touch(tile, carry):
        at = pl.ds(pl.multiple_of(tile * BLOCK, BLOCK), BLOCK)
        row, strength = rows[:, at], stiff[:, at]
        strength = jnp.where(row >= 0, strength, 0.0)
        spot = row & (BLOCK - 1)
        own = row < BLOCK
        total = jnp.sum(strength, 0, keepdims=True)
        partner = partner_s[tile]
        for part in range(3):
            mine = state[part, pl.ds(tile, 1), :]
            theirs = state[part, pl.ds(partner, 1), :]
            found = jnp.where(
                own,
                lanes_at(jnp.broadcast_to(mine, row.shape), spot),
                lanes_at(jnp.broadcast_to(theirs, row.shape), spot),
            )
            contact[part, pl.ds(tile, 1), :] = total * mine - jnp.sum(strength * found, 0, keepdims=True)
        return carry

    w_down.wait_recv()
    w_up.wait_recv()
    share = tiles // ITERS
    for sweep in range(1, ITERS + 1):
        for plane in range(1, planes - 1):
            relax(sweep, plane)
        down, up = exchanges[sweep - 1]
        up.wait_recv()
        relax(sweep, 0)
        exchanges[sweep][0].start()
        down.wait_recv()
        relax(sweep, planes - 1)
        exchanges[sweep][1].start()
        lax.fori_loop((sweep - 1) * share, sweep * share, touch, 0)

    def keep(kind, plane, values):
        for part in range(per_row):
            fields[(kind * planes + plane) * per_row + part] = values[:, part * BLOCK : (part + 1) * BLOCK]

    def gradient(plane):
        here = pbuf[ITERS, plane, PAD : PAD + slab, :]
        after = pbuf[ITERS, plane, PAD + 1 : PAD + slab + 1, :]
        before = pbuf[ITERS, plane, PAD - 1 : PAD + slab - 1, :]
        keep(1, plane, 0.5 * (after - before))
        keep(2, plane, 0.5 * (after_z(here) - before_z(here)))

    for plane in range(planes):
        gradient(plane)
    keep_ids.wait()
    for copy in exchanges[ITERS]:
        copy.wait_recv()
    for plane in range(planes):
        keep(0, plane, 0.5 * (above(ITERS, plane) - below(ITERS, plane)))

    def take_block(block, part_ref, tile):
        plane, row, quarter = block // (width_y * per_row), (block // per_row) % width_y, block % per_row
        here = (row // half) == core
        row = jnp.clip(row - first_y, 0, slab - 1)
        for kind in range(4):
            found = fields[(kind * planes + plane) * per_row + quarter, pl.ds(row, 1), :]
            part_ref[kind, pl.ds(tile, 1), :] = jnp.where(here, found, 0.0)

    def take_tile(tile, carry):
        take_block(ids_sib[0, tile], part_sent, tile)
        return carry

    def take_own(tile, carry):
        take_block(tile_s[tile], part_own, tile)
        return carry

    lax.fori_loop(0, tiles, take_tile, 0)
    give = remote(18, part_sent, part_got, sibling)
    give.start()
    lax.fori_loop(0, tiles, take_own, 0)
    give.wait_recv()

    def finish(step, carry):
        first = pl.multiple_of(step * 8, 8)
        at = pl.ds(first, 8)
        slot = first * BLOCK + iota((8, BLOCK), 0) * BLOCK + iota((8, BLOCK), 1)
        live = slot < count
        where = cell[at, :]
        found = [lanes_at(part_own[kind, at, :] + part_got[kind, at, :], where) for kind in range(4)]
        vol8, drag8 = vol[at, :], drag[at, :]
        scale = TIME_STEP / vol8
        for part in range(3):
            slope, old = found[part], velocity[part, at, :]
            force = contact[part, at, :] - vol8 * slope + drag8 * (-slope * found[3] - old)
            out[part, at, :] = jnp.where(live, old + scale * force, 0.0)
        return carry

    lax.fori_loop(0, tiles // 8, finish, 0)

    sent = [to_sibling, to_across, passed_on, id_sibling, id_across, id_passed, w_down, w_up, give]
    for copy in sent + [copy for pair in exchanges for copy in pair]:
        copy.wait_send()


def on_device(
    grain_pos, grain_vel, grain_vol, drag_coef, grain_count, contact_rows, contact_stiff, partner_block, halo_list,
    grain_cell, tile_cell_block, pressure_old, pressure_source, solid_old,
):
    tiles = grain_vol.shape[0] // BLOCK
    planes, width_y, width_z = pressure_old.shape
    slab = width_y // 2 + GHOST
    halo_blocks = halo_list.shape[1] // BLOCK
    blocked = lambda flat: flat.reshape(tiles, BLOCK)
    vmem, smem, far = (pl.BlockSpec(memory_space=space) for space in (pltpu.VMEM, pltpu.SMEM, pl.ANY))
    copies = 9 + 2 * (ITERS + 1)
    out = pl.pallas_call(
        kernel,
        out_shape=jax.ShapeDtypeStruct((3, tiles, BLOCK), F32),
        in_specs=[smem] * 3 + [vmem] * 9 + [far] * 3,
        out_specs=vmem,
        scratch_shapes=[
            pltpu.VMEM((4, tiles, 2 * BLOCK), F32),
            pltpu.VMEM((4, 1, tiles), jnp.int32),
            pltpu.SMEM((1, tiles), jnp.int32),
            pltpu.VMEM((3, tiles + 2 * halo_blocks, BLOCK), F32),
            pltpu.VMEM((3, tiles, BLOCK), F32),
            pltpu.VMEM((2 * halo_blocks, BLOCK), jnp.int32),
            pltpu.VMEM((2, 3, halo_blocks, BLOCK), F32),
            pltpu.VMEM((3, tiles, BLOCK), F32),
            pltpu.VMEM((ITERS + 1, planes, slab + 2 * PAD, width_z), F32),
            pltpu.VMEM((ITERS + 1, 2, slab, width_z), F32),
            pltpu.VMEM((planes, slab, width_z), F32),
            pltpu.VMEM((planes, slab, width_z), F32),
            pltpu.VMEM((planes, slab, width_z), F32),
            pltpu.VMEM((planes, slab, width_z), F32),
            pltpu.VMEM((4 * planes * width_z // BLOCK, slab, BLOCK), F32),
            pltpu.VMEM((4, tiles, BLOCK), F32),
            pltpu.VMEM((4, tiles, BLOCK), F32),
            pltpu.VMEM((4, tiles, BLOCK), F32),
            pltpu.SemaphoreType.DMA((copies,)),
            pltpu.SemaphoreType.DMA((copies,)),
            pltpu.SemaphoreType.DMA((4,)),
        ],
        compiler_params=pltpu.CompilerParams(
            collective_id=0, has_side_effects=True, vmem_limit_bytes=56 * 1024 * 1024
        ),
        name="step",
    )(
        grain_count, partner_block, tile_cell_block, tile_cell_block.reshape(1, tiles), grain_pos, grain_vel,
        blocked(grain_vol), blocked(drag_coef), blocked(grain_cell), contact_rows, contact_stiff, halo_list,
        pressure_old, pressure_source, solid_old,
    )
    return out.reshape(3, tiles * BLOCK)


def solution(mesh):
    flat, wide = P(("grp", "reg")), P(None, ("grp", "reg"))
    field = P("reg", None, None)
    return jax.shard_map(
        on_device,
        mesh=mesh,
        in_specs=(wide, wide, flat, flat, flat, wide, wide, flat, wide, flat, flat, field, field, field),
        out_specs=wide,
        check_vma=False,
    )
```

time: 312 us -> 71.5 us (0.23)
  the two profiles are of different devices: /device:TPU:32 before, /device:TPU:1 now
where the time goes in v1:
time: 71.5 us; the launch traced here: 70.3 us
  Pallas kernels  67.9 us (95%)
  local copies, waits for them, and re-layouts  1.77 us (2%)
    pallas_call x1, Pallas kernels, on_device(): pl.pallas_call(kernel, out_shape=jax.ShapeDtypeStruct((3, tiles, BLOCK),...  67.9 us
    unnamed x1, local copies, waits for them, and re-layouts  1.77 us

profile of v1, /device:TPU:1, one launch (start us, length us, event | category | flops | bytes accessed | tf_op | source)
XLA Modules:
  0.0 70.3 jit_solution(2436684716573973203)
XLA Ops:
  0.7 67.9 %step.1 = f32[3,128,128]{2,1,0:T(8,128)} custom-call(s32[1]{0:T(128)S(6)} %copy.18.count_s, s32[128]{0:T(128)} %partner_s.1, s32[128]{0:T(128)} %tile_s.1, s32[1,128]{1,0:T(1,128)} %bitcast.12, f32[3,16384]{1,0:T(4,128)} %pos.1, f32[3,16384]{1,0:T(4,128)} %vel.1, f32[128,128]{1,0:T(8,128)} %bitcast.9, f32[128,128]{1,0:T(8,128)} %bitcast.10, ...), custom_call_target="tpu_custom_call" | custom-call | tf_op jit(solution)/shard_map/step/pallas_call | solution.py:348
  68.6 1.8 %copy.17 = f32[1,3,128,128]{3,1,2,0:T(4,128)} copy(f32[1,3,128,128]{3,2,1,0:T(8,128)} %bitcast.8) | data formatting | bytes 393216

commit v2 on v1

--- a/solution.py
+++ b/solution.py
@@ -35,7 +35,7 @@
 def kernel(
     count_s, partner_s, tile_s, tile_v, pos, vel, vol, drag, cell, rows, stiff, halo, p_old, source, solid_old,
     out,
-    loads, ids_all, ids_sib, state, velocity, halo_row, halo_out, contact, pbuf, hbuf, src_v, old_v, coef_a, coef_b,
+    loads, ids_all, ids_sib, state, velocity, halo_out, contact, pbuf, hbuf, src_v, old_v, coef_a, coef_b,
     fields, part_own, part_sent, part_got, send, recv, local,
 ):
     tiles, slot_count = vol.shape[0], rows.shape[0]
@@ -133,33 +133,30 @@
             velocity[part, pl.ds(tile, 1), :] = moved[part : part + 1]
         return carry
 
-    lax.fori_loop(0, tiles, tabulate, 0)
-
-    def halo_rows(block, carry):
-        at = pl.ds(pl.multiple_of(block * BLOCK, BLOCK), BLOCK)
+    lax.fori_loop(0, tiles, tabulate, 0, unroll=4)
+
+    pieces = []
+    for part in range(3):
+        high, low = split(state[part, 0:tiles, :].T)
+        pieces.append(jnp.concatenate([high, low], 1))
+    table = jnp.concatenate(pieces, 0)
+    pair = 2 * BLOCK
+
+    def pick(step, carry):
+        at = pl.ds(pl.multiple_of(step * pair, pair), pair)
         for side in range(2):
-            halo_row[pl.ds(block + side * halo_blocks, 1), :] = halo[side : side + 1, at]
-        return carry
-
-    lax.fori_loop(0, halo_blocks, halo_rows, 0)
-    wanted = halo_row[...]
-    wanted_row, wanted_lane = wanted >> 7, wanted & (BLOCK - 1)
-
-    def pick(row, picked):
-        here = wanted_row == row
-        return tuple(
-            jnp.where(
-                here,
-                lanes_at(jnp.broadcast_to(state[part, pl.ds(row, 1), :], wanted.shape), wanted_lane),
-                picked[part],
-            )
-            for part in range(3)
-        )
-
-    picked = lax.fori_loop(0, tiles, pick, tuple(jnp.zeros(wanted.shape, F32) for _ in range(3)))
-    for part in range(3):
-        for side in range(2):
-            halo_out[side, part] = picked[part][side * halo_blocks : (side + 1) * halo_blocks]
+            wanted = halo[side : side + 1, at]
+            hot = ((iota((2 * tiles, pair), 0) & (tiles - 1)) == (wanted >> 7)).astype(F32).astype(BF16)
+            found = jnp.dot(table, hot, preferred_element_type=F32)
+            here = iota((BLOCK, pair), 0) == (wanted & (BLOCK - 1))
+            for part in range(3):
+                chosen = jnp.where(here, found[part * BLOCK : (part + 1) * BLOCK], 0.0)
+                chosen = jnp.sum(chosen, 0, keepdims=True)
+                halo_out[side, part, pl.ds(2 * step, 1), :] = chosen[:, :BLOCK]
+                halo_out[side, part, pl.ds(2 * step + 1, 1), :] = chosen[:, BLOCK:]
+        return carry
+
+    lax.fori_loop(0, halo_blocks // 2, pick, 0)
     w_down = remote(16, halo_out.at[0], state.at[:, pl.ds(tiles + halo_blocks, halo_blocks), :], lower)
     w_up = remote(17, halo_out.at[1], state.at[:, pl.ds(tiles, halo_blocks), :], upper)
     w_down.start()
@@ -175,6 +172,7 @@
             pbuf[sweep, plane, 0:PAD, :] = jnp.zeros((PAD, width_z), F32)
             pbuf[sweep, plane, PAD + slab : 2 * PAD + slab, :] = jnp.zeros((PAD, width_z), F32)
 
+    fields[:, slab : slab + PAD, :] = jnp.zeros((4 * planes * per_row, PAD, BLOCK), F32)
     id_sibling.wait_recv()
     keep_ids = pltpu.make_async_copy(ids_all.at[1], ids_sib, local.at[3])
     keep_ids.start()
@@ -209,7 +207,7 @@
             driving = src_v[plane, :, at] + solid - old_v[plane, :, at]
             coef_a[plane, :, at] = driving * inverse
             coef_b[plane, :, at] = porous * inverse
-            fields[(3 * planes + plane) * per_row + part] = 1.0 / (porous + dragged)
+            fields[(3 * planes + plane) * per_row + part, 0:slab] = 1.0 / (porous + dragged)
 
     lane = iota((slab, width_z), 1)
 
@@ -269,11 +267,11 @@
         down.wait_recv()
         relax(sweep, planes - 1)
         exchanges[sweep][1].start()
-        lax.fori_loop((sweep - 1) * share, sweep * share, touch, 0)
+        lax.fori_loop((sweep - 1) * share, sweep * share, touch, 0, unroll=4)
 
     def keep(kind, plane, values):
         for part in range(per_row):
-            fields[(kind * planes + plane) * per_row + part] = values[:, part * BLOCK : (part + 1) * BLOCK]
+            fields[(kind * planes + plane) * per_row + part, 0:slab] = values[:, part * BLOCK : (part + 1) * BLOCK]
 
     def gradient(plane):
         here = pbuf[ITERS, plane, PAD : PAD + slab, :]
@@ -290,13 +288,14 @@
     for plane in range(planes):
         keep(0, plane, 0.5 * (above(ITERS, plane) - below(ITERS, plane)))
 
+    bits_z, bits_y = per_row.bit_length() - 1, width_y.bit_length() - 1
+
     def take_block(block, part_ref, tile):
-        plane, row, quarter = block // (width_y * per_row), (block // per_row) % width_y, block % per_row
-        here = (row // half) == core
-        row = jnp.clip(row - first_y, 0, slab - 1)
+        quarter, row = block & (per_row - 1), (block >> bits_z) & (width_y - 1)
+        plane = block >> (bits_z + bits_y)
+        row = jnp.where((row >= half) == (core > 0), row - first_y, slab)
         for kind in range(4):
-            found = fields[(kind * planes + plane) * per_row + quarter, pl.ds(row, 1), :]
-            part_ref[kind, pl.ds(tile, 1), :] = jnp.where(here, found, 0.0)
+            part_ref[kind, pl.ds(tile, 1), :] = fields[kind * planes * per_row + plane * per_row + quarter, pl.ds(row, 1), :]
 
     def take_tile(tile, carry):
         take_block(ids_sib[0, tile], part_sent, tile)
@@ -306,10 +305,10 @@
         take_block(tile_s[tile], part_own, tile)
         return carry
 
-    lax.fori_loop(0, tiles, take_tile, 0)
+    lax.fori_loop(0, tiles, take_tile, 0, unroll=8)
     give = remote(18, part_sent, part_got, sibling)
     give.start()
-    lax.fori_loop(0, tiles, take_own, 0)
+    lax.fori_loop(0, tiles, take_own, 0, unroll=8)
     give.wait_recv()
 
     def finish(step, carry):
@@ -324,10 +323,13 @@
         for part in range(3):
             slope, old = found[part], velocity[part, at, :]
             force = contact[part, at, :] - vol8 * slope + drag8 * (-slope * found[3] - old)
-            out[part, at, :] = jnp.where(live, old + scale * force, 0.0)
-        return carry
-
-    lax.fori_loop(0, tiles // 8, finish, 0)
+            new = jnp.where(live, old + scale * force, 0.0)
+            for tile in range(8):
+                lanes = pl.ds(pl.multiple_of((first + tile) * BLOCK, BLOCK), BLOCK)
+                out[part : part + 1, lanes] = new[tile : tile + 1]
+        return carry
+
+    lax.fori_loop(0, tiles // 8, finish, 0, unroll=2)
 
     sent = [to_sibling, to_across, passed_on, id_sibling, id_across, id_passed, w_down, w_up, give]
     for copy in sent + [copy for pair in exchanges for copy in pair]:
@@ -347,7 +349,7 @@
     copies = 9 + 2 * (ITERS + 1)
     out = pl.pallas_call(
         kernel,
-        out_shape=jax.ShapeDtypeStruct((3, tiles, BLOCK), F32),
+        out_shape=jax.ShapeDtypeStruct((3, tiles * BLOCK), F32),
         in_specs=[smem] * 3 + [vmem] * 9 + [far] * 3,
         out_specs=vmem,
         scratch_shapes=[
@@ -356,7 +358,6 @@
             pltpu.SMEM((1, tiles), jnp.int32),
             pltpu.VMEM((3, tiles + 2 * halo_blocks, BLOCK), F32),
             pltpu.VMEM((3, tiles, BLOCK), F32),
-            pltpu.VMEM((2 * halo_blocks, BLOCK), jnp.int32),
             pltpu.VMEM((2, 3, halo_blocks, BLOCK), F32),
             pltpu.VMEM((3, tiles, BLOCK), F32),
             pltpu.VMEM((ITERS + 1, planes, slab + 2 * PAD, width_z), F32),
@@ -365,7 +366,7 @@
             pltpu.VMEM((planes, slab, width_z), F32),
             pltpu.VMEM((planes, slab, width_z), F32),
             pltpu.VMEM((planes, slab, width_z), F32),
-            pltpu.VMEM((4 * planes * width_z // BLOCK, slab, BLOCK), F32),
+            pltpu.VMEM((4 * planes * width_z // BLOCK, slab + PAD, BLOCK), F32),
             pltpu.VMEM((4, tiles, BLOCK), F32),
             pltpu.VMEM((4, tiles, BLOCK), F32),
             pltpu.VMEM((4, tiles, BLOCK), F32),
@@ -382,7 +383,7 @@
         blocked(grain_vol), blocked(drag_coef), blocked(grain_cell), contact_rows, contact_stiff, halo_list,
         pressure_old, pressure_source, solid_old,
     )
-    return out.reshape(3, tiles * BLOCK)
+    return out
 
 
 def solution(mesh):

time: 71.5 us -> 54.6 us (0.76); the launches traced: 70.3 us -> 54.4 us
  Pallas kernels: 67.9 us -> 52.1 us
    pallas_call x1, Pallas kernels: 67.9 us -> 52.1 us  [on_device(): pl.pallas_call(kernel, out_shape=jax.ShapeDtypeStruct((3, tiles * BLOCK),...]
where the time goes in v2:
time: 54.6 us; the launch traced here: 54.4 us
  Pallas kernels  52.1 us (95%)
  local copies, waits for them, and re-layouts  1.7 us (3%)
  between operations  0.66 us (1%)
    pallas_call x1, Pallas kernels, on_device(): pl.pallas_call(kernel, out_shape=jax.ShapeDtypeStruct((3, tiles * BLOCK),...  52.1 us
    unnamed x1, local copies, waits for them, and re-layouts  1.7 us

profile of v2, /device:TPU:1, one launch (start us, length us, event | category | flops | bytes accessed | tf_op | source)
XLA Modules:
  0.0 54.4 jit_solution(6041638064169986413)
XLA Ops:
  0.7 52.1 %step.1 = f32[3,16384]{1,0:T(4,128)} custom-call(s32[1]{0:T(128)S(6)} %copy.16.count_s, s32[128]{0:T(128)} %partner_s.1, s32[128]{0:T(128)} %tile_s.1, s32[1,128]{1,0:T(1,128)} %bitcast.7, f32[3,16384]{1,0:T(4,128)} %pos.1, f32[3,16384]{1,0:T(4,128)} %vel.1, f32[128,128]{1,0:T(8,128)} %bitcast.4, f32[128,128]{1,0:T(8,128)} %bitcast.5, s32[128,128]{1,0:T(8,128)} %bitcast.6, ...), custom_call_target="tpu_custom_call" | custom-call | tf_op jit(solution)/shard_map/step/pallas_call | solution.py:350
  52.7 1.7 %copy.17 = f32[3,16384]{1,0:T(4,128)} copy(f32[3,16384]{1,0:T(4,128)} %step.1) | data formatting | bytes 393216

commit v3 on v2

v3 whole, which is shorter than its diff:
```python
import functools

import jax
import jax.numpy as jnp
from jax import lax
from jax.experimental import pallas as pl
from jax.experimental.pallas import tpu as pltpu
from jax.sharding import PartitionSpec as P

BLOCK = 128
ITERS = 4
SPRING = 1.0
DAMPING = 0.5
TIME_STEP = 0.5
GHOST = 8
PAD = 8
MESH = pl.DeviceIdType.MESH
F32 = jnp.float32
BF16 = jnp.bfloat16


def iota(shape, axis):
    return lax.broadcasted_iota(jnp.int32, shape, axis)


def split(values):
    high = values.astype(BF16)
    return high, (values - high.astype(F32)).astype(BF16)


def lanes_at(table, lane):
    return jnp.take_along_axis(table, lane, axis=1, mode="promise_in_bounds")


def kernel(
    count_s, partner_s, tile_s, tile_v, vol, drag, cell, halo, pos_far, vel_far, rows_far, stiff_far, p_old, source, solid_old,
    out,
    pos, vel, rows, stiff, loads, ids_all, ids_sib, state, velocity, halo_out, contact, pbuf, near, deep, edge, src_v, old_v,
    coef, coef_got, fields, part_own, part_sent, part_got, send, recv, local,
):
    tiles, slot_count = vol.shape[0], rows.shape[0]
    planes, width_y, width_z = p_old.shape
    half = width_y // 2
    slab = half + GHOST
    per_row = width_z // BLOCK
    halo_blocks = halo.shape[1] // BLOCK
    group, region = lax.axis_index("grp"), lax.axis_index("reg")
    groups, regions = lax.axis_size("grp"), lax.axis_size("reg")
    core = lax.rem(group, 2)
    sibling_at, across_at = group + 1 - 2 * core, lax.rem(group + 2, groups)
    passed_at = lax.rem(sibling_at + 2, groups)
    sibling, across = {"grp": sibling_at}, {"grp": across_at}
    upper = {"reg": lax.rem(region + 1, regions)}
    lower = {"reg": lax.rem(region + regions - 1, regions)}
    has_lower, has_upper = region > 0, region < regions - 1
    last = groups - 1
    first_y = pl.multiple_of(core * (half - GHOST), 8)
    count = count_s[0]

    def remote(index, src, dst, device):
        return pltpu.make_async_remote_copy(
            src_ref=src, dst_ref=dst, send_sem=send.at[index], recv_sem=recv.at[index],
            device_id=device, device_id_type=MESH,
        )

    def greet(device):
        pl.semaphore_signal(barrier, inc=1, device_id=device, device_id_type=MESH)

    barrier = pltpu.get_barrier_semaphore()
    greet(sibling)
    greet(across)
    pl.when(has_lower)(lambda: greet(lower))
    pl.when(has_upper)(lambda: greet(upper))

    inner = pl.ds(PAD, slab)
    rows_y = pl.ds(first_y, slab)
    fetches = [
        pltpu.make_async_copy(src, dst, local.at[index])
        for index, (src, dst) in enumerate(
            [
                (pos_far, pos),
                (vel_far, vel),
                (p_old.at[:, rows_y, :], pbuf.at[0, :, inner, :]),
                (source.at[:, rows_y, :], src_v),
                (solid_old.at[:, rows_y, :], old_v),
                (rows_far, rows),
                (stiff_far, stiff),
            ]
        )
    ]
    for copy in fetches:
        copy.start()

    cells = iota((BLOCK, BLOCK), 0)

    def deposit(step, carry):
        first = pl.multiple_of(step * 8, 8)
        cell8 = cell[pl.ds(first, 8), :]
        slot = first * BLOCK + iota((8, BLOCK), 0) * BLOCK + iota((8, BLOCK), 1)
        live = slot < count
        vol8 = jnp.where(live, vol[pl.ds(first, 8), :], 0.0)
        drag8 = jnp.where(live, drag[pl.ds(first, 8), :], 0.0)
        both = jnp.concatenate([vol8, drag8], 0)
        high, low = split(both)
        pieces = jnp.concatenate([high, low], 0)
        total = jnp.zeros((32, BLOCK), F32)
        for tile in range(8):
            hot = (cell8[tile : tile + 1, :] == cells).astype(F32).astype(BF16)
            found = lax.dot_general(pieces, hot, (((1,), (1,)), ((), ())), preferred_element_type=F32)
            total = jnp.where(iota((32, BLOCK), 0) % 8 == tile, found, total)
        total = total[:16] + total[16:]
        loads[0, pl.ds(first, 8), 0:BLOCK] = total[:8]
        loads[0, pl.ds(first, 8), BLOCK : 2 * BLOCK] = total[8:]
        return carry

    lax.fori_loop(0, tiles // 8, deposit, 0)
    ids_all[0] = tile_v[...]
    pl.semaphore_wait(barrier, 2 + jnp.where(has_lower, 1, 0) + jnp.where(has_upper, 1, 0))

    to_sibling = remote(0, loads.at[0], loads.at[1], sibling)
    to_across = remote(1, loads.at[0], loads.at[2], across)
    passed_on = remote(2, loads.at[2], loads.at[3], sibling)
    id_sibling = remote(3, tile_v, ids_all.at[1], sibling)
    id_across = remote(4, tile_v, ids_all.at[2], across)
    id_passed = remote(5, ids_all.at[2], ids_all.at[3], sibling)

    def start(*copies):
        for copy in copies:
            copy.start()

    def arrive(*copies):
        for copy in copies:
            copy.wait_recv()

    def leave(*copies):
        for copy in copies:
            copy.wait_send()

    def blank(slot):
        loads[slot] = jnp.zeros((tiles, 2 * BLOCK), F32)
        ids_all[slot] = jnp.zeros((1, tiles), jnp.int32)

    sends = group != last
    pl.when(sends)(lambda: start(id_across, to_across, id_sibling, to_sibling))

    def planes_out(sweep):
        if sweep == 0:
            low, high = p_old.at[0, rows_y, :], p_old.at[planes - 1, rows_y, :]
        else:
            low, high = pbuf.at[sweep, 0, inner, :], pbuf.at[sweep, planes - 1, inner, :]
        return remote(6 + 2 * sweep, low, near.at[sweep, 1], lower), remote(7 + 2 * sweep, high, near.at[sweep, 0], upper)

    exchanges = [planes_out(sweep) for sweep in range(ITERS - 1)]
    deep_down = remote(12, pbuf.at[ITERS - 1, 0:2, inner, :], deep.at[1, :, inner, :], lower)
    deep_up = remote(13, pbuf.at[ITERS - 1, planes - 2 : planes, inner, :], deep.at[0, :, inner, :], upper)
    coef_down = remote(14, coef.at[0], coef_got.at[1], lower)
    coef_up = remote(15, coef.at[planes - 1], coef_got.at[0], upper)
    w_down = remote(16, halo_out.at[0], state.at[:, pl.ds(tiles + halo_blocks, halo_blocks), :], lower)
    w_up = remote(17, halo_out.at[1], state.at[:, pl.ds(tiles, halo_blocks), :], upper)
    pl.when(has_lower)(lambda: start(exchanges[0][0]))
    pl.when(has_upper)(lambda: start(exchanges[0][1]))
    fetches[0].wait()
    fetches[1].wait()

    def tabulate(tile, carry):
        at = pl.ds(pl.multiple_of(tile * BLOCK, BLOCK), BLOCK)
        moved = vel[:, at]
        mixed = SPRING * pos[:, at] - DAMPING * moved
        for part in range(3):
            state[part, pl.ds(tile, 1), :] = mixed[part : part + 1]
            velocity[part, pl.ds(tile, 1), :] = moved[part : part + 1]
        return carry

    lax.fori_loop(0, tiles, tabulate, 0, unroll=4)

    pieces = []
    for part in range(3):
        high, low = split(state[part, 0:tiles, :].T)
        pieces.append(jnp.concatenate([high, low], 1))
    table = jnp.concatenate(pieces, 0)
    pair = 2 * BLOCK

    def pick(step, carry):
        at = pl.ds(pl.multiple_of(step * pair, pair), pair)
        for side in range(2):
            wanted = halo[side : side + 1, at]
            hot = ((iota((2 * tiles, pair), 0) & (tiles - 1)) == (wanted >> 7)).astype(F32).astype(BF16)
            found = jnp.dot(table, hot, preferred_element_type=F32)
            here = iota((BLOCK, pair), 0) == (wanted & (BLOCK - 1))
            for part in range(3):
                chosen = jnp.where(here, found[part * BLOCK : (part + 1) * BLOCK], 0.0)
                chosen = jnp.sum(chosen, 0, keepdims=True)
                halo_out[side, part, pl.ds(2 * step, 1), :] = chosen[:, :BLOCK]
                halo_out[side, part, pl.ds(2 * step + 1, 1), :] = chosen[:, BLOCK:]
        return carry

    lax.fori_loop(0, halo_blocks // 2, pick, 0)
    pl.when(has_lower)(lambda: start(w_down))
    pl.when(has_upper)(lambda: start(w_up))

    @pl.when(across_at != last)
    def _():
        arrive(id_across, to_across)
        start(id_passed, passed_on)

    pl.when(across_at == last)(lambda: blank(2))
    pl.when(sibling_at == last)(lambda: blank(1))
    pl.when(passed_at == last)(lambda: blank(3))
    zero_rows = jnp.zeros((PAD, width_z), F32)
    for sweep in range(ITERS + 1):
        for plane in range(planes):
            pbuf[sweep, plane, 0:PAD, :] = zero_rows
            pbuf[sweep, plane, PAD + slab : 2 * PAD + slab, :] = zero_rows
    for side in range(2):
        for plane in range(2):
            deep[side, plane, 0:PAD, :] = zero_rows
            deep[side, plane, PAD + slab : 2 * PAD + slab, :] = zero_rows
    fields[:, slab : slab + PAD, :] = jnp.zeros((4 * planes * per_row, PAD, BLOCK), F32)

    def outside(side):
        for sweep in range(ITERS - 1):
            near[sweep, side] = jnp.zeros((slab, width_z), F32)
        for plane in range(2):
            deep[side, plane, PAD : PAD + slab, :] = jnp.zeros((slab, width_z), F32)
        edge[side] = jnp.zeros((slab, width_z), F32)
        at = pl.ds(tiles + side * halo_blocks, halo_blocks)
        state[:, at, :] = jnp.zeros((3, halo_blocks, BLOCK), F32)

    pl.when(jnp.logical_not(has_lower))(lambda: outside(0))
    pl.when(jnp.logical_not(has_upper))(lambda: outside(1))

    keep_ids = pltpu.make_async_copy(ids_all.at[1], ids_sib, local.at[7])

    @pl.when(sibling_at != last)
    def _():
        arrive(id_sibling)
        keep_ids.start()
        arrive(to_sibling)

    pl.when(passed_at != last)(lambda: arrive(id_passed, passed_on))
    for copy in fetches[2:5]:
        copy.wait()

    every = loads[...].reshape(4 * tiles, 2 * BLOCK)
    high, low = split(every)
    both = jnp.concatenate([high, low], 1)
    ids = jnp.concatenate([ids_all[source_id] for source_id in range(4)], 1)
    block_of = (iota((slab, 4 * tiles), 0) + first_y) * per_row

    def place(plane):
        hot = jnp.concatenate(
            [
                (block_of + (plane * width_y * per_row + part) == ids).astype(F32).astype(BF16)
                for part in range(per_row)
            ],
            0,
        )
        placed = jnp.dot(hot, both, preferred_element_type=F32)
        placed = placed[:, : 2 * BLOCK] + placed[:, 2 * BLOCK :]
        for part in range(per_row):
            at = slice(part * BLOCK, (part + 1) * BLOCK)
            solid = placed[part * slab : (part + 1) * slab, :BLOCK]
            dragged = placed[part * slab : (part + 1) * slab, BLOCK:]
            porous = 1.0 / (1.0 + solid)
            inverse = 1.0 / (6.0 * porous + dragged + 1.0)
            driving = src_v[plane, :, at] + solid - old_v[plane, :, at]
            coef[plane, 0, :, at] = driving * inverse
            coef[plane, 1, :, at] = porous * inverse
            fields[(3 * planes + plane) * per_row + part, 0:slab] = 1.0 / (porous + dragged)

    lane = iota((slab, width_z), 1)

    def before_z(values):
        return jnp.where(lane == 0, 0.0, pltpu.roll(values, 1, 1))

    def after_z(values):
        return jnp.where(lane == width_z - 1, 0.0, pltpu.roll(values, width_z - 1, 1))

    def middle(sweep, plane):
        if 0 <= plane < planes:
            return pbuf[sweep, plane, PAD : PAD + slab, :]
        if sweep < ITERS - 1:
            return near[sweep, 0 if plane < 0 else 1]
        if sweep == ITERS:
            return edge[0 if plane < 0 else 1]
        side, place_in = (0, plane + 2) if plane < 0 else (1, plane - planes)
        return deep[side, place_in, PAD : PAD + slab, :]

    def relax(sweep, plane):
        old = sweep - 1
        if 0 <= plane < planes:
            home, mine = pbuf.at[old, plane], coef.at[plane]
        else:
            home = deep.at[0, 1] if plane < 0 else deep.at[1, 0]
            mine = coef_got.at[0 if plane < 0 else 1]
        here = home[PAD : PAD + slab, :]
        total = middle(old, plane - 1) + middle(old, plane + 1)
        total = total + home[PAD - 1 : PAD + slab - 1, :] + home[PAD + 1 : PAD + slab + 1, :]
        total = total + before_z(here) + after_z(here)
        relaxed = mine[0] + mine[1] * total
        if 0 <= plane < planes:
            pbuf[sweep, plane, PAD : PAD + slab, :] = relaxed
        else:
            edge[0 if plane < 0 else 1] = relaxed

    def touch(tile, carry):
        at = pl.ds(pl.multiple_of(tile * BLOCK, BLOCK), BLOCK)
        row, strength = rows[:, at], stiff[:, at]
        strength = jnp.where(row >= 0, strength, 0.0)
        spot = row & (BLOCK - 1)
        own = row < BLOCK
        total = jnp.sum(strength, 0, keepdims=True)
        partner = partner_s[tile]
        for part in range(3):
            mine = state[part, pl.ds(tile, 1), :]
            theirs = state[part, pl.ds(partner, 1), :]
            found = jnp.where(
                own,
                lanes_at(jnp.broadcast_to(mine, row.shape), spot),
                lanes_at(jnp.broadcast_to(theirs, row.shape), spot),
            )
            contact[part, pl.ds(tile, 1), :] = total * mine - jnp.sum(strength * found, 0, keepdims=True)
        return carry

    def touches(step, carry):
        for tile in range(4):
            touch(4 * step + tile, carry)
        return carry

    top = planes - 1

    def ends(sweep):
        down, up = exchanges[sweep - 1]
        pl.when(has_lower)(lambda: arrive(up))
        relax(sweep, 0)
        if sweep < ITERS - 1:
            pl.when(has_lower)(lambda: start(exchanges[sweep][0]))
        pl.when(has_upper)(lambda: arrive(down))
        relax(sweep, top)
        if sweep < ITERS - 1:
            pl.when(has_upper)(lambda: start(exchanges[sweep][1]))

    def inside(sweep):
        for plane in range(1, top):
            relax(sweep, plane)

    share = tiles // (ITERS - 1)
    shares = [0, share // 2, tiles // 2, tiles]

    def contacts(step):
        lax.fori_loop(shares[step - 1] // 4, shares[step] // 4, touches, 0)

    place(0)
    place(top)
    ends(1)
    pl.when(has_lower)(lambda: start(coef_down))
    pl.when(has_upper)(lambda: start(coef_up))
    for plane in range(1, top):
        place(plane)
    inside(1)
    fetches[5].wait()
    fetches[6].wait()
    pl.when(has_lower)(lambda: arrive(w_up))
    pl.when(has_upper)(lambda: arrive(w_down))
    contacts(1)
    ends(2)
    inside(2)
    contacts(2)
    inside(3)
    ends(3)
    pl.when(has_lower)(lambda: start(deep_down))
    pl.when(has_upper)(lambda: start(deep_up))
    inside(4)
    contacts(3)

    def keep(kind, plane, values):
        for part in range(per_row):
            fields[(kind * planes + plane) * per_row + part, 0:slab] = values[:, part * BLOCK : (part + 1) * BLOCK]

    def gradient(plane):
        here = pbuf[ITERS, plane, PAD : PAD + slab, :]
        after = pbuf[ITERS, plane, PAD + 1 : PAD + slab + 1, :]
        before = pbuf[ITERS, plane, PAD - 1 : PAD + slab - 1, :]
        keep(1, plane, 0.5 * (after - before))
        keep(2, plane, 0.5 * (after_z(here) - before_z(here)))

    for plane in range(1, top):
        gradient(plane)

    @pl.when(has_lower)
    def _():
        arrive(deep_up, coef_up)
        relax(ITERS, -1)

    relax(ITERS, 0)

    @pl.when(has_upper)
    def _():
        arrive(deep_down, coef_down)
        relax(ITERS, planes)

    relax(ITERS, top)
    gradient(0)
    gradient(top)
    for plane in range(planes):
        keep(0, plane, 0.5 * (middle(ITERS, plane + 1) - middle(ITERS, plane - 1)))

    bits_z, bits_y = per_row.bit_length() - 1, width_y.bit_length() - 1

    def take_block(block, part_ref, tile):
        quarter, row = block & (per_row - 1), (block >> bits_z) & (width_y - 1)
        plane = block >> (bits_z + bits_y)
        row = jnp.where((row >= half) == (core > 0), row - first_y, slab)
        for kind in range(4):
            part_ref[kind, pl.ds(tile, 1), :] = fields[kind * planes * per_row + plane * per_row + quarter, pl.ds(row, 1), :]

    def take_tile(tile, carry):
        take_block(ids_sib[0, tile], part_sent, tile)
        return carry

    def take_own(tile, carry):
        take_block(tile_s[tile], part_own, tile)
        return carry

    give = remote(18, part_sent, part_got, sibling)

    @pl.when(sibling_at != last)
    def _():
        keep_ids.wait()
        lax.fori_loop(0, tiles, take_tile, 0, unroll=8)
        give.start()

    lax.fori_loop(0, tiles, take_own, 0, unroll=8)
    pl.when(sends)(lambda: arrive(give))

    def finish(step, carry):
        first = pl.multiple_of(step * 8, 8)
        at = pl.ds(first, 8)
        slot = first * BLOCK + iota((8, BLOCK), 0) * BLOCK + iota((8, BLOCK), 1)
        live = slot < count
        where = cell[at, :]
        found = [lanes_at(part_own[kind, at, :] + part_got[kind, at, :], where) for kind in range(4)]
        vol8, drag8 = vol[at, :], drag[at, :]
        scale = TIME_STEP / vol8
        for part in range(3):
            slope, old = found[part], velocity[part, at, :]
            force = contact[part, at, :] - vol8 * slope + drag8 * (-slope * found[3] - old)
            new = jnp.where(live, scale * force, -old)
            for tile in range(8):
                lanes = pl.ds(pl.multiple_of((first + tile) * BLOCK, BLOCK), BLOCK)
                out[part : part + 1, lanes] = new[tile : tile + 1]
        return carry

    lax.fori_loop(0, tiles // 8, finish, 0, unroll=2)

    pl.when(sends)(lambda: leave(id_across, to_across, id_sibling, to_sibling))
    pl.when(across_at != last)(lambda: leave(id_passed, passed_on))
    pl.when(sibling_at != last)(lambda: leave(give))
    pl.when(has_lower)(lambda: leave(*[down for down, up in exchanges], deep_down, coef_down, w_down))
    pl.when(has_upper)(lambda: leave(*[up for down, up in exchanges], deep_up, coef_up, w_up))


def on_device(
    grain_pos, grain_vel, grain_vol, drag_coef, grain_count, contact_rows, contact_stiff, partner_block, halo_list,
    grain_cell, tile_cell_block, pressure_old, pressure_source, solid_old,
):
    tiles = grain_vol.shape[0] // BLOCK
    planes, width_y, width_z = pressure_old.shape
    slab = width_y // 2 + GHOST
    halo_blocks = halo_list.shape[1] // BLOCK
    blocked = lambda flat: flat.reshape(tiles, BLOCK)
    vmem, smem, far = (pl.BlockSpec(memory_space=space) for space in (pltpu.VMEM, pltpu.SMEM, pl.ANY))
    copies = 19
    sheet = (slab, width_z)
    scratch = [
        ((3, tiles * BLOCK), F32),
        ((3, tiles * BLOCK), F32),
        (contact_rows.shape, jnp.int32),
        (contact_rows.shape, F32),
        ((4, tiles, 2 * BLOCK), F32),
        ((4, 1, tiles), jnp.int32),
        None,
        ((3, tiles + 2 * halo_blocks, BLOCK), F32),
        ((3, tiles, BLOCK), F32),
        ((2, 3, halo_blocks, BLOCK), F32),
        ((3, tiles, BLOCK), F32),
        ((ITERS + 1, planes, slab + 2 * PAD, width_z), F32),
        ((ITERS - 1, 2) + sheet, F32),
        ((2, 2, slab + 2 * PAD, width_z), F32),
        ((2,) + sheet, F32),
        ((planes,) + sheet, F32),
        ((planes,) + sheet, F32),
        ((planes, 2) + sheet, F32),
        ((2, 2) + sheet, F32),
        ((4 * planes * width_z // BLOCK, slab + PAD, BLOCK), F32),
        ((4, tiles, BLOCK), F32),
        ((4, tiles, BLOCK), F32),
        ((4, tiles, BLOCK), F32),
    ]
    change = pl.pallas_call(
        kernel,
        out_shape=jax.ShapeDtypeStruct((3, tiles * BLOCK), F32),
        in_specs=[smem] * 3 + [vmem] * 5 + [far] * 7,
        out_specs=vmem,
        scratch_shapes=[pltpu.SMEM((1, tiles), jnp.int32) if one is None else pltpu.VMEM(*one) for one in scratch]
        + [pltpu.SemaphoreType.DMA((copies,)), pltpu.SemaphoreType.DMA((copies,)), pltpu.SemaphoreType.DMA((8,))],
        compiler_params=pltpu.CompilerParams(
            collective_id=0, has_side_effects=True, vmem_limit_bytes=56 * 1024 * 1024
        ),
        name="step",
    )(
        grain_count, partner_block, tile_cell_block, tile_cell_block.reshape(1, tiles),
        blocked(grain_vol), blocked(drag_coef), blocked(grain_cell), halo_list, grain_pos, grain_vel,
        contact_rows, contact_stiff, pressure_old, pressure_source, solid_old,
    )
    return grain_vel + change


def solution(mesh):
    flat, wide = P(("grp", "reg")), P(None, ("grp", "reg"))
    field = P("reg", None, None)
    return jax.shard_map(
        on_device,
        mesh=mesh,
        in_specs=(wide, wide, flat, flat, flat, wide, wide, flat, wide, flat, flat, field, field, field),
        out_specs=wide,
        check_vma=False,
    )
```

time: 54.6 us -> 47.1 us (0.86)
  the two profiles are of different devices: /device:TPU:1 before, /device:TPU:89 now
where the time goes in v3:
time: 47.1 us; the launch traced here: 46.9 us
  Pallas kernels  44.5 us (94%)
  other arithmetic  1.72 us (4%)
  between operations  0.68 us (1%)
    pallas_call x1, Pallas kernels, on_device(): pl.pallas_call(kernel, out_shape=jax.ShapeDtypeStruct((3, tiles * BLOCK),...  44.5 us
    add x1, other arithmetic, on_device(): return grain_vel + change  1.72 us

profile of v3, /device:TPU:89, one launch (start us, length us, event | category | flops | bytes accessed | tf_op | source)
XLA Modules:
  0.0 46.9 jit_solution(2692177261763454473)
XLA Ops:
  0.7 0.0 copy-start
  0.7 44.5 %step.1 = f32[3,16384]{1,0:T(4,128)} custom-call(s32[1]{0:T(128)S(6)} %copy.15.count_s, s32[128]{0:T(128)} %partner_s.1, s32[128]{0:T(128)} %tile_s.1, s32[1,128]{1,0:T(1,128)} %bitcast.7, f32[128,128]{1,0:T(8,128)} %bitcast.4, f32[128,128]{1,0:T(8,128)} %bitcast.5, s32[128,128]{1,0:T(8,128)} %bitcast.6, s32[2,4096]{1,0:T(2,128)} %halo.1, ...), custom_call_target="tpu_custom_call" | custom-call | tf_op jit(solution)/shard_map/step/pallas_call | solution.py:500
  45.2 0.0 copy-done
  45.2 1.7 %add.3 = f32[3,16384]{1,0:T(4,128)} add(f32[3,16384]{1,0:T(4,128)S(1)} %copy-done, f32[3,16384]{1,0:T(4,128)} %step.1) | non-fusion elementwise | flops 49152 | bytes 589824 | tf_op jit(solution)/shard_map/add | solution.py:516
Async XLA Ops:
  0.7 44.6 %copy-start = (f32[3,16384]{1,0:T(4,128)S(1)}, f32[3,16384]{1,0:T(4,128)}, u32[]{:S(2)}) copy-start(f32[3,16384]{1,0:T(4,128)} %vel_far.1) | copy-start | bytes 589828
